TPU v7x, 128 devices: a whole 4x4x4 slice. The times are simulated.
128 devices in a mesh: ty: 16 (over x, z), tx: 8 (over y, core).
Axes of the slice: x: 4, y: 4, z: 4, core: 2. Of those that a mesh axis runs over, the one named last changes fastest.
Arguments:
- screen: float32 [1024, 2048], P('ty', 'tx'), may hold values from -6 to 6
- wind_table: float32 [2, 16], replicated, may hold values from -0.4 to 0.4
- wind_index: int32 [16, 8], P('ty', 'tx'), may hold values from 0 to 15
- tile_id: int32 [16, 8, 8, 32, 1], P('ty', 'tx'), may hold values from 0 to 127; in each aligned block of 256 rows (0 to 255, 256 to 511, ..., all dimensions but the last counted through in order) at most 4 rows name the same one
- cell_index: int32 [16, 8, 8, 32], P('ty', 'tx'), may hold values from 0 to 8000
- fractions: float32 [2, 16, 8, 8, 32], P(None, 'ty', 'tx'), may hold values from 0 to 1
Outputs:
- screen_next: float32 [1024, 2048], P('ty', 'tx')
- phases: float32 [16, 8, 8, 32, 128], P('ty', 'tx')
- slopes: float32 [16, 8, 8, 32, 128], P('ty', 'tx')
Inputs may be any that keep to these rules, and one draw needn't show every extreme that they name: `tile_id`: among the 256 records of one station group and direction group, at most 4 name the same tile, a bound that some block reaches of them.
All inputs are finite; a program needn't handle non-finite values.
Results may differ from a plain program's by a relative error of at most 0.0003.
Values sent between devices are 32-bit elements; how exact they have to be, the bound alone decides.
No kernel may reach another device: no remote copies, remote signals or barrier semaphores. Data moves between devices by JAX's collectives and lax.ppermute only.
A program may use at most 64 MiB of HBM per device.

v0:
```python
import jax
import jax.numpy as jnp
from jax import lax
from jax.sharding import PartitionSpec as P

P_SIZE = 128
SUB = 4


DIFFUSION = 0.2


def padded_2(cells, sides, width):
    for axis, dim in sides:
        count = lax.axis_size(axis)
        ends = count - 1
        head = lax.slice_in_dim(cells, 0, width, axis=dim)
        tail = lax.slice_in_dim(cells, cells.shape[dim] - width, cells.shape[dim], axis=dim)
        cells = jnp.concatenate(
            [
                lax.ppermute(tail, axis, [(i, (i + 1) % count) for i in range(ends)]),
                cells,
                lax.ppermute(head, axis, [((i + 1) % count, i) for i in range(ends)]),
            ],
            axis=dim,
        )
    return cells


def mix(center, east_side, west_side, south_side, north_side, wind_east, wind_south):
    advect = wind_east * (east_side - west_side) + wind_south * (south_side - north_side)
    spread = east_side + west_side + south_side + north_side - 4.0 * center
    return center - 0.5 * advect + DIFFUSION * spread


def strip_values(upper_row, lower_row, frac_row, frac_col):
    left_up = upper_row[..., :-1]
    right_up = upper_row[..., 1:]
    left_low = lower_row[..., :-1]
    right_low = lower_row[..., 1:]
    upper_mix = (1.0 - frac_col) * left_up + frac_col * right_up
    lower_mix = (1.0 - frac_col) * left_low + frac_col * right_low
    phase_vals = (1.0 - frac_row) * upper_mix + frac_row * lower_mix
    slope_vals = (1.0 - frac_col) * (left_low - left_up) + frac_col * (right_low - right_up)
    return (phase_vals, slope_vals)


def choose_entry(table_row, position):
    return jnp.sum(jnp.where(jnp.arange(table_row.shape[0]) == position, table_row, 0.0))


def lookup(field, requests):
    leading = requests.shape[:-1]
    flat = requests.reshape(-1, 3)
    cells_flat = flat[:, 0].astype(jnp.int32)
    col_total = field.shape[1]
    span_cols = col_total - P_SIZE - 1
    row_start = cells_flat // span_cols
    col_start = cells_flat % span_cols
    flat_field = field.reshape(-1)
    base_index = row_start * col_total + col_start
    offsets = jnp.arange(P_SIZE + 1, dtype=jnp.int32)
    upper_index = base_index[:, None] + offsets[None, :]
    upper_row = jnp.take(flat_field, upper_index, axis=0)
    lower_row = jnp.take(flat_field, upper_index + col_total, axis=0)
    phase_vals, slope_vals = strip_values(upper_row, lower_row, flat[:, 1:2], flat[:, 2:3])
    stacked = jnp.stack([phase_vals, slope_vals], axis=1)
    return stacked.reshape(leading + (2, P_SIZE))


def local(screen, wind_table, wind_index, tile_id, cell_index, fractions):
    tile_rows = lax.axis_size("ty")
    tile_cols = lax.axis_size("tx")
    tile_total = tile_rows * tile_cols
    wind_east = choose_entry(wind_table[0], wind_index[0, 0])
    wind_south = choose_entry(wind_table[1], wind_index[0, 0])
    field = screen
    for substep in range(SUB):
        padded = padded_2(field, (("ty", 0), ("tx", 1)), 1)
        field = mix(
            padded[1:-1, 1:-1],
            padded[1:-1, 2:],
            padded[1:-1, :-2],
            padded[2:, 1:-1],
            padded[:-2, 1:-1],
            wind_east,
            wind_south,
        )
    record_count = tile_id.shape[2] * tile_id.shape[3]
    capacity = max(2, 2 * record_count // tile_total)
    target = tile_id.reshape(-1)
    order = jnp.argsort(target, stable=True)
    sorted_target = target[order]
    tile_line = jnp.arange(tile_total)
    counts = jnp.sum((target[:, None] == tile_line[None, :]).astype(jnp.int32), axis=0)
    starts = jnp.cumsum(counts) - counts
    sorted_start = jnp.sum(
        jnp.where(sorted_target[:, None] == tile_line[None, :], starts[None, :], 0), axis=1
    )
    rank_sorted = jnp.arange(record_count) - sorted_start
    rank = jnp.zeros((record_count,), jnp.int32).at[order].set(rank_sorted)
    slot = target * capacity + rank
    record_values = jnp.stack(
        [
            cell_index.reshape(-1).astype(jnp.float32),
            fractions[0].reshape(-1),
            fractions[1].reshape(-1),
        ],
        axis=1,
    )
    requests = jnp.zeros((tile_total * capacity, 3), jnp.float32).at[slot].set(record_values)
    requests = requests.reshape(tile_total, capacity, 3)
    returned = lax.all_to_all(
        lookup(
            field, lax.all_to_all(requests, ("ty", "tx"), split_axis=0, concat_axis=0, tiled=True)
        ),
        ("ty", "tx"),
        split_axis=0,
        concat_axis=0,
        tiled=True,
    )
    gathered = returned.reshape(tile_total * capacity, 2, P_SIZE)[slot]
    out_shape = (1, 1, tile_id.shape[2], tile_id.shape[3], P_SIZE)
    phases = gathered[:, 0].reshape(out_shape)
    slopes = gathered[:, 1].reshape(out_shape)
    return (field, phases, slopes)


def solution(mesh):
    in_specs = (
        P("ty", "tx"),
        P(),
        P("ty", "tx"),
        P("ty", "tx", None, None, None),
        P("ty", "tx", None, None),
        P(None, "ty", "tx", None, None),
    )
    out_specs = (P("ty", "tx"), P("ty", "tx", None, None, None), P("ty", "tx", None, None, None))
    return jax.shard_map(local, mesh=mesh, in_specs=in_specs, out_specs=out_specs, check_vma=False)
```

profile of v0, /device:TPU:1, one launch (start us, length us, event | category | flops | bytes accessed | tf_op | source)
XLA Modules:
  0.0 809.1 jit_solution(6178070391496223444)
XLA Ops:
  2.7 5.0 collective-permute-start
  10.4 3.2 sort.17
  14.3 1.4 fusion.3
  16.0 2.9 collective-permute-start.2
  18.8 3.2 collective-permute-start.3
  22.3 1.9 gather_fusion
  27.0 4.2 collective-permute-start.4
  32.0 2.1 collective-permute-start.6
  34.1 3.8 collective-permute-start.7
  42.0 4.5 collective-permute-start.8
  47.4 2.0 collective-permute-start.10
  49.4 4.7 collective-permute-start.11
  57.9 5.5 collective-permute-start.12
  64.2 1.9 collective-permute-start.14
  66.1 5.1 collective-permute-start.15
  72.5 1.6 copy.32
  74.0 18.0 %all-to-all-start = ((f32[128,4,3]{1,2,0:T(4,128)}), f32[128,4,3]{1,2,0:T(4,128)S(1)}, u32[]{:S(2)}, u32[]{:S(2)}) async-start(f32[128,4,3]{1,2,0:T(4,128)} %copy.32), calls=%async_computation | async-start | bytes 524288 | tf_op jit(solution)/shard_map/all_to_all | solution.py:115
  92.2 1.4 fusion.17
  93.6 9.2 %all-to-all-done = f32[128,4,3]{1,2,0:T(4,128)S(1)} async-done(((f32[128,4,3]{1,2,0:T(4,128)}), f32[128,4,3]{1,2,0:T(4,128)S(1)}, u32[]{:S(2)}, u32[]{:S(2)}) %all-to-all-start) | async-done | bytes 6176 | tf_op jit(solution)/shard_map/all_to_all | solution.py:115
  105.1 339.1 %gather_fusion.2 = f32[66048]{0:T(1024)S(1)} fusion(f32[16384]{0:T(1024)S(1)} %bitcast.34, s32[66560]{0:T(1024)S(1)} %pad_clamp_fusion.1), kind=kCustom, calls=%fused_computation.clone | custom fusion | bytes 792576 | tf_op jit(solution)/shard_map/jit(_take)/gather | solution.py:64
  446.0 339.1 %gather_fusion.3 = f32[66048]{0:T(1024)S(1)} fusion(f32[16384]{0:T(1024)S(1)} %bitcast.35, s32[66560]{0:T(1024)S(1)} %pad_clamp_fusion), kind=kCustom, calls=%fused_computation.1.clone | custom fusion | bytes 792576 | tf_op jit(solution)/shard_map/jit(_take)/gather | solution.py:65
  788.9 4.8 all-to-all-start.1
  794.4 2.0 multiply_add_fusion.2
  796.4 10.8 %all-to-all-done.1 = f32[128,4,2,128]{3,2,1,0:T(2,128)S(1)} async-done(((f32[128,4,2,128]{3,2,1,0:T(2,128)}), f32[128,4,2,128]{3,2,1,0:T(2,128)S(1)}, u32[]{:S(2)}, u32[]{:S(2)}) %all-to-all-start.1) | async-done | bytes 524320 | tf_op jit(solution)/shard_map/all_to_all | solution.py:113
  (120 shorter events, 29.8 us)
Async XLA Ops:
  0.6 15.2 %copy-start.4 = (f32[64,256]{1,0:T(8,128)S(1)}, f32[64,256]{1,0:T(8,128)}, u32[]{:S(2)}) copy-start(f32[64,256]{1,0:T(8,128)} %param.8) | copy-start | bytes 196612
  1.4 14.4 %collective-permute-start.1 = (f32[1,256]{1,0:T(1,128)S(1)}, f32[1,256]{1,0:T(1,128)S(1)}, u32[]{:S(2)}, u32[]{:S(2)}) collective-permute-start(f32[1,256]{1,0:T(1,128)S(1)} %get-tuple-element.27), channel_id=1, source_target_pairs={{8,0},{16,8},{24,16},{32,24},{40,32},{48,40},{56,48},{64,56},{72,6... | collective-permute-start | bytes 3080 | tf_op jit(solution)/shard_map/ppermute | solution.py:23
  2.7 13.2 %collective-permute-start = (f32[1,256]{1,0:T(1,128)S(1)}, f32[1,256]{1,0:T(1,128)S(1)}, u32[]{:S(2)}, u32[]{:S(2)}) collective-permute-start(f32[1,256]{1,0:T(1,128)S(1)} %get-tuple-element.26), channel_id=1, source_target_pairs={{0,8},{8,16},{16,24},{24,32},{32,40},{40,48},{48,56},{56,64},{64,7... | collective-permute-start | bytes 3080 | tf_op jit(solution)/shard_map/ppermute | solution.py:21
  16.0 8.3 %collective-permute-start.2 = (f32[66,1]{1,0:T(8,128)S(1)}, f32[66,1]{1,0:T(8,128)S(1)}, u32[]{:S(2)}, u32[]{:S(2)}) collective-permute-start(f32[66,1]{1,0:T(8,128)S(1)} %get-tuple-element.19), channel_id=1, source_target_pairs={{1,0},{2,1},{3,2},{4,3},{5,4},{6,5},{7,6},{9,8},{10,9},{11,10},{12... | collective-permute-start | bytes 800 | tf_op jit(solution)/shard_map/ppermute | solution.py:23
  18.8 5.5 collective-permute-start.3
  25.7 5.7 collective-permute-start.5
  27.0 4.9 collective-permute-start.4
  32.0 7.3 collective-permute-start.6
  34.1 5.2 collective-permute-start.7
  40.7 5.9 collective-permute-start.9
  42.0 5.2 collective-permute-start.8
  46.6 24.7 %copy-start.19 = (s32[256]{0:T(256)}, s32[256]{0:T(256)S(1)}, u32[]{:S(2)}) copy-start(s32[256]{0:T(256)S(1)} %compare_select_fusion.2) | copy-start | bytes 3076
  47.4 6.8 copy-start.21
  47.4 6.9 collective-permute-start.10
  49.4 5.7 collective-permute-start.11
  56.5 35.6 %copy-start.2 = (f32[64,256]{1,0:T(8,128)}, f32[64,256]{1,0:T(8,128)S(1)}, u32[]{:S(2)}) copy-start(f32[64,256]{1,0:T(8,128)S(1)} %multiply_add_fusion.3) | copy-start | bytes 196612
  56.6 7.0 collective-permute-start.13
  57.9 6.3 collective-permute-start.12
  63.6 28.5 %copy-start.11 = (f32[1,256]{1,0:T(1,128)}, f32[1,256]{1,0:T(1,128)S(1)}, u32[]{:S(2)}) copy-start(f32[1,256]{1,0:T(1,128)S(1)} %collective-permute-done.13) | copy-start | bytes 3076
  64.1 28.0 %copy-start.13 = (f32[1,256]{1,0:T(1,128)}, f32[1,256]{1,0:T(1,128)S(1)}, u32[]{:S(2)}) copy-start(f32[1,256]{1,0:T(1,128)S(1)} %collective-permute-done.12) | copy-start | bytes 3076
  64.2 27.9 %collective-permute-start.14 = (f32[66,1]{1,0:T(8,128)S(1)}, f32[66,1]{1,0:T(8,128)S(1)}, u32[]{:S(2)}, u32[]{:S(2)}) collective-permute-start(f32[66,1]{1,0:T(8,128)S(1)} %get-tuple-element.13), channel_id=1, source_target_pairs={{1,0},{2,1},{3,2},{4,3},{5,4},{6,5},{7,6},{9,8},{10,9},{11,10},{12... | collective-permute-start | bytes 800 | tf_op jit(solution)/shard_map/ppermute | solution.py:23
  66.1 26.0 %collective-permute-start.15 = (f32[66,1]{1,0:T(8,128)S(1)}, f32[66,1]{1,0:T(8,128)S(1)}, u32[]{:S(2)}, u32[]{:S(2)}) collective-permute-start(f32[66,1]{1,0:T(8,128)S(1)} %get-tuple-element.12), channel_id=1, source_target_pairs={{0,1},{1,2},{2,3},{3,4},{4,5},{5,6},{6,7},{8,9},{9,10},{10,11},{11... | collective-permute-start | bytes 800 | tf_op jit(solution)/shard_map/ppermute | solution.py:21
  74.0 28.8 %all-to-all-start = ((f32[128,4,3]{1,2,0:T(4,128)}), f32[128,4,3]{1,2,0:T(4,128)S(1)}, u32[]{:S(2)}, u32[]{:S(2)}) async-start(f32[128,4,3]{1,2,0:T(4,128)} %copy.32), calls=%async_computation | async-start | bytes 524288 | tf_op jit(solution)/shard_map/all_to_all | solution.py:115
  788.9 18.3 %all-to-all-start.1 = ((f32[128,4,2,128]{3,2,1,0:T(2,128)}), f32[128,4,2,128]{3,2,1,0:T(2,128)S(1)}, u32[]{:S(2)}, u32[]{:S(2)}) async-start(f32[128,4,2,128]{3,2,1,0:T(2,128)} %pad_maximum_fusion), calls=%async_computation.1 | async-start | bytes 1048576 | tf_op jit(solution)/shard_map/all_to_all | solution.py:113
  (16 other events, 30.2 us)
where the time goes:
time: 810 us; the launch traced here: 809 us
  local copies, waits for them, and re-layouts  694 us (86%)
  starting transfers between devices  72.8 us (9%)
  waiting for transfers between devices  22.6 us (3%)
  other arithmetic  18 us (2%)
    gather x2, local copies, waits for them, and re-layouts, lookup(): upper_row = jnp.take(flat_field, upper_index, axis=0)  340 us
    gather x2, local copies, waits for them, and re-layouts, lookup(): lower_row = jnp.take(flat_field, upper_index + col_total, axis=0)  340 us
    ppermute x8, starting transfers between devices, padded_2(): lax.ppermute(tail, axis, [(i, (i + 1) % count) for i in range(ends)])  36 us
    all_to_all x1, starting transfers between devices, local(): lax.all_to_all(requests, ('ty', 'tx'), split_axis=0, concat_axis=0, tiled...  18 us
  transfers between devices with their start and end apart: 18, of which 6 were waited for; matrix products, arithmetic and copies ran while one was open for 2% of the time, Pallas kernels for 0%

commit v1 on v0

v1 whole, which is shorter than its diff:
```python
import jax
import jax.numpy as jnp
from jax import lax
from jax.experimental import pallas as pl
from jax.experimental.pallas import tpu as pltpu
from jax.sharding import PartitionSpec as P

RY = 64
RX = 256
P_SIZE = 128
SPAN = RX - P_SIZE - 1
SUB = 4
CAP = 4
DIFFUSION = 0.2

REC = 64
F32 = jnp.float32
BF16 = jnp.bfloat16
VMEM = pl.BlockSpec(memory_space=pltpu.VMEM)
SMEM = pl.BlockSpec(memory_space=pltpu.SMEM)


def iota(shape, dim):
    return lax.broadcasted_iota(jnp.int32, shape, dim)


def three_terms(x):
    high = x.astype(BF16)
    rest = x - high.astype(F32)
    middle = rest.astype(BF16)
    low = (rest - middle.astype(F32)).astype(BF16)
    return high, middle, low


def request_kernel(
    n_tx, screen_ref, table_ref, index_ref, tile_ref, cell_ref, frac_ref,
    send_ref, top_ref, bottom_ref, slot_ref,
):
    tx = lax.axis_index("tx")
    groups, width = tile_ref.shape[0], tile_ref.shape[2]
    records = groups * width
    tiles = send_ref.shape[0] // SUB
    top_ref[...] = screen_ref[0:8, :]
    bottom_ref[...] = screen_ref[RY - 8 : RY, :]

    def flat(rows):
        return jnp.concatenate(rows, axis=1)

    tile = flat([tile_ref[s] for s in range(groups)])
    cell = flat([cell_ref[s : s + 1, :] for s in range(groups)]).astype(F32)
    frac_row = flat([frac_ref[0, s : s + 1, :] for s in range(groups)])
    frac_col = flat([frac_ref[1, s : s + 1, :] for s in range(groups)])

    names = jnp.where(iota((tiles, records), 0) == tile, 1.0, 0.0)
    before = (iota((records, records), 0) < iota((records, records), 1)).astype(F32).astype(BF16)
    earlier = jnp.dot(names.astype(BF16), before, preferred_element_type=F32)
    rank = jnp.sum(names * earlier, axis=0, keepdims=True)
    slot_ref[...] = tile * (2 * CAP) + 2 * rank.astype(jnp.int32)

    picks = jnp.concatenate(
        [jnp.where(earlier == k, names, 0.0).astype(BF16) for k in range(CAP)], axis=0
    )
    line = iota((128, records), 0)
    values = jnp.where(
        line == REC,
        cell,
        jnp.where(line == REC + 1, frac_row, jnp.where(line == REC + 2, frac_col, 0.0)),
    )
    found = sum(
        lax.dot_general(picks, part, (((1,), (1,)), ((), ())), preferred_element_type=F32)
        for part in three_terms(values)
    )
    requests = found[0:tiles]
    for k in range(1, CAP):
        requests = requests + pltpu.roll(found[k * tiles : (k + 1) * tiles], 4 * k, axis=1)

    chosen = jnp.where(iota((2, table_ref.shape[1]), 1) == index_ref[...], table_ref[...], 0.0)
    wind = jnp.sum(chosen, axis=1, keepdims=True)
    lane = iota((1, 128), 1)
    winds = jnp.where(lane == REC, wind[0:1], jnp.where(lane == REC + 1, wind[1:2], 0.0))

    blank = jnp.zeros((128 - RY, 128), F32)
    west_cols = jnp.concatenate([screen_ref[:, 0:128], blank], axis=0).T
    east_cols = jnp.concatenate([screen_ref[:, RX - 128 : RX], blank], axis=0).T
    to_east = lax.rem(iota((tiles, 128), 0), n_tx) == tx + 1
    for c in range(SUB):
        row = jnp.where(
            to_east, east_cols[128 - SUB + c : 129 - SUB + c, :], west_cols[c : c + 1, :]
        )
        if c == 0:
            row = row + requests
        if c == 1:
            row = row + winds
        send_ref[pl.ds(c, tiles, stride=SUB), :] = row


def sample_kernel(
    n_ty, n_tx, screen_ref, north_ref, south_ref, got_ref, next_ref, reply_ref, edge_ref
):
    ty, tx = lax.axis_index("ty"), lax.axis_index("tx")
    tiles = n_ty * n_tx

    def chunk(dy, dx):
        y = jnp.clip(ty + dy, 0, n_ty - 1)
        x = jnp.clip(tx + dx, 0, n_tx - 1)
        return [got_ref[pl.ds((y * n_tx + x) * SUB + c, 1), :] for c in range(SUB)]

    around = {(dy, dx): chunk(dy, dx) for dy in (-1, 0, 1) for dx in (-1, 0, 1)}

    lane = iota((1, 128), 1)
    edge_ref[...] = jnp.zeros((128, 128), F32)
    for dx, start in ((1, 0), (-1, 128 - SUB)):
        for c in range(SUB):
            below = pltpu.roll(around[1, dx][c], RY, axis=1)
            above = pltpu.roll(around[-1, dx][c], 2 * SUB, axis=1)
            edge_ref[start + c : start + c + 1, :] = jnp.where(
                lane < RY, around[0, dx][c], jnp.where(lane < RY + SUB, below, above)
            )
    sides = edge_ref[...].T[0 : RY + 2 * SUB]

    rows, cols = RY + 2 * SUB, RX + 128
    ends = jnp.where(iota((2 * SUB, RX), 0) < SUB, south_ref[...], north_ref[...])
    field = jnp.concatenate(
        [jnp.concatenate([screen_ref[...], ends], axis=0), sides], axis=1
    )
    row, col = iota((rows, cols), 0), iota((rows, cols), 1)
    no_south, no_north = ty == n_ty - 1, ty == 0
    no_east, no_west = tx == n_tx - 1, tx == 0
    first_south = jnp.where(no_south, RY, RY + SUB)
    last_north = jnp.where(no_north, rows, RY + SUB)
    first_east = jnp.where(no_east, RX, RX + REC)
    last_west = jnp.where(no_west, cols, RX + REC)
    inside = ((row < first_south) | (row >= last_north)) & ((col < first_east) | (col >= last_west))

    def spread_wind(which):
        def line(dy):
            w = [around[dy, dx][1][:, REC + which : REC + which + 1] for dx in (0, 1, -1)]
            c = iota((1, cols), 1)
            return jnp.where(c < RX, w[0], jnp.where(c < RX + REC, w[1], w[2]))

        return jnp.where(row < RY, line(0), jnp.where(row < RY + SUB, line(1), line(-1)))

    wind_east, wind_south = spread_wind(0), spread_wind(1)
    field = jnp.where(inside, field, 0.0)
    for _ in range(SUB):
        east, west = pltpu.roll(field, cols - 1, axis=1), pltpu.roll(field, 1, axis=1)
        south, north = pltpu.roll(field, rows - 1, axis=0), pltpu.roll(field, 1, axis=0)
        advect = wind_east * (east - west) + wind_south * (south - north)
        spread = east + west + south + north - 4.0 * field
        field = jnp.where(inside, field - 0.5 * advect + DIFFUSION * spread, 0.0)
    tile = field[0:RY, 0:RX]
    next_ref[...] = tile

    parts = jnp.concatenate(three_terms(tile), axis=0)
    records = got_ref[pl.ds(0, tiles, stride=SUB), :]
    start_row = jnp.floor((records + 0.5) * (1.0 / SPAN))
    start_col = (records - SPAN * start_row).astype(jnp.int32)
    line = lax.rem(iota((tiles, 3 * RY), 1), RY).astype(F32)
    lanes = iota((tiles, 128), 1)
    for k in range(CAP):
        at = REC + 4 * k
        row_k, col_k = start_row[:, at : at + 1], start_col[:, at : at + 1]
        frac_row, frac_col = records[:, at + 1 : at + 2], records[:, at + 2 : at + 3]
        upper = jnp.dot(
            jnp.where(line == row_k, 1.0, 0.0).astype(BF16), parts, preferred_element_type=F32
        )
        lower = jnp.dot(
            jnp.where(line == row_k + 1.0, 1.0, 0.0).astype(BF16), parts, preferred_element_type=F32
        )
        spot = lanes + col_k
        near = spot < 128
        spot = spot & 127
        for p, value in enumerate(((1.0 - frac_row) * upper + frac_row * lower, lower - upper)):
            value = (1.0 - frac_col) * value + frac_col * pltpu.roll(value, RX - 1, axis=1)
            strip = jnp.where(
                near,
                jnp.take_along_axis(value[:, 0:128], spot, axis=1),
                jnp.take_along_axis(value[:, 128:256], spot, axis=1),
            )
            reply_ref[pl.ds(2 * k + p, tiles, stride=2 * CAP), :] = strip


def collect_kernel(slot_ref, got_ref, phase_ref, slope_ref):
    def step(n, carry):
        slot = slot_ref[0, n]
        phase_ref[pl.ds(n, 1), :] = got_ref[pl.ds(slot, 1), :]
        slope_ref[pl.ds(n, 1), :] = got_ref[pl.ds(slot + 1, 1), :]
        return carry

    lax.fori_loop(0, phase_ref.shape[0], step, 0, unroll=8)


def local(screen, wind_table, wind_index, tile_id, cell_index, fractions):
    n_ty, n_tx = lax.axis_size("ty"), lax.axis_size("tx")
    tiles = n_ty * n_tx
    groups, width = tile_id.shape[2], tile_id.shape[3]
    records = groups * width

    def shaped(*shape, dtype=F32):
        return jax.ShapeDtypeStruct(shape, dtype)

    send, top, bottom, slots = pl.pallas_call(
        lambda *refs: request_kernel(n_tx, *refs),
        out_shape=(
            shaped(tiles * SUB, 128),
            shaped(8, RX),
            shaped(8, RX),
            shaped(1, records, dtype=jnp.int32),
        ),
        in_specs=[VMEM] * 6,
        out_specs=(VMEM,) * 4,
        name="make_requests",
    )(
        screen,
        wind_table,
        wind_index,
        tile_id.reshape(groups, 1, width),
        cell_index.reshape(groups, width),
        fractions.reshape(2, groups, width),
    )

    def exchange(x):
        return lax.all_to_all(x, ("ty", "tx"), split_axis=0, concat_axis=0, tiled=True)

    got = exchange(send)
    north = lax.ppermute(bottom, "ty", [(i, i + 1) for i in range(n_ty - 1)])
    south = lax.ppermute(top, "ty", [(i + 1, i) for i in range(n_ty - 1)])
    screen_next, reply = pl.pallas_call(
        lambda *refs: sample_kernel(n_ty, n_tx, *refs),
        out_shape=(shaped(RY, RX), shaped(tiles * 2 * CAP, 128)),
        in_specs=[VMEM] * 4,
        out_specs=(VMEM,) * 2,
        scratch_shapes=[pltpu.VMEM((128, 128), F32)],
        name="step_and_sample",
    )(screen, north, south, got)
    returned = exchange(reply)
    phases, slopes = pl.pallas_call(
        collect_kernel,
        out_shape=(shaped(records, P_SIZE),) * 2,
        in_specs=[SMEM, VMEM],
        out_specs=(VMEM,) * 2,
        name="collect",
    )(slots, returned)
    out_shape = (1, 1, groups, width, P_SIZE)
    return screen_next, phases.reshape(out_shape), slopes.reshape(out_shape)


def solution(mesh):
    in_specs = (
        P("ty", "tx"),
        P(),
        P("ty", "tx"),
        P("ty", "tx", None, None, None),
        P("ty", "tx", None, None),
        P(None, "ty", "tx", None, None),
    )
    out_specs = (P("ty", "tx"), P("ty", "tx", None, None, None), P("ty", "tx", None, None, None))
    return jax.shard_map(local, mesh=mesh, in_specs=in_specs, out_specs=out_specs, check_vma=False)
```

time: 810 us -> 56.1 us (0.07)
  local copies, waits for them, and re-layouts: 694 us -> 0.71 us
  starting transfers between devices: 72.8 us -> 16.2 us
  blocking collectives: 0 us -> 22.6 us
  other arithmetic: 18 us -> 0 us
  waiting for transfers between devices: 22.6 us -> 6.02 us
  Pallas kernels: 0 us -> 8.87 us
    gather x6 -> x0, local copies, waits for them, and re-layouts: 683 us -> none  [the longest x2 340 us: lookup(): upper_row = jnp.take(flat_field, upper_index, axis=0)]
    ppermute x16 -> x2, starting transfers between devices: 50 us -> 4.7 us  [the longest x1 3.41 us: local(): north = lax.ppermute(bottom, 'ty', [(i, i + 1) for i in range(n_ty - 1)])]
    all_to_all x0 -> x1, blocking collectives: none -> 22.6 us  [exchange(): lax.all_to_all(x, ('ty', 'tx'), split_axis=0, concat_axis=0, tiled=True)]
    all_to_all x2 -> x1, waiting for transfers between devices: 20 us -> 2.51 us  [exchange(): lax.all_to_all(x, ('ty', 'tx'), split_axis=0, concat_axis=0, tiled=True)]
    all_to_all x2 -> x1, starting transfers between devices: 22.8 us -> 11.5 us  [exchange(): lax.all_to_all(x, ('ty', 'tx'), split_axis=0, concat_axis=0, tiled=True)]
    pallas_call x0 -> x3, Pallas kernels: none -> 8.87 us  [the longest x1 4.37 us: local(): pl.pallas_call(lambda *refs: sample_kernel(n_ty, n_tx, *refs), out_shape=...]
  transfers between devices with their start and end apart: 18 -> 3, of which waited for: 6 -> 2; matrix products, arithmetic and copies ran while one was open for 2% -> 0% of each run, Pallas kernels for 0% -> 0%
where the time goes in v1:
time: 56.1 us; the launch traced here: 55.7 us
  blocking collectives  22.6 us (40%)
  starting transfers between devices  16.2 us (29%)
  Pallas kernels  8.87 us (16%)
  waiting for transfers between devices  6.02 us (11%)
  between operations  1.34 us (2%)
  local copies, waits for them, and re-layouts  0.71 us (1%)
    all_to_all x1, blocking collectives, exchange(): lax.all_to_all(x, ('ty', 'tx'), split_axis=0, concat_axis=0, tiled=True)  22.6 us
    all_to_all x1, starting transfers between devices, exchange(): lax.all_to_all(x, ('ty', 'tx'), split_axis=0, concat_axis=0, tiled=True)  11.5 us
    pallas_call x1, Pallas kernels, local(): pl.pallas_call(lambda *refs: sample_kernel(n_ty, n_tx, *refs), out_shape=...  4.37 us
    ppermute x1, waiting for transfers between devices, local(): south = lax.ppermute(top, 'ty', [(i + 1, i) for i in range(n_ty - 1)])  3.51 us
    ppermute x1, starting transfers between devices, local(): north = lax.ppermute(bottom, 'ty', [(i, i + 1) for i in range(n_ty - 1)])  3.41 us
    all_to_all x1, waiting for transfers between devices, exchange(): lax.all_to_all(x, ('ty', 'tx'), split_axis=0, concat_axis=0, tiled=True)  2.51 us
    pallas_call x1, Pallas kernels, local(): pl.pallas_call(lambda *refs: request_kernel(n_tx, *refs), out_shape=(shap...  2.26 us
    pallas_call x1, Pallas kernels, local(): pl.pallas_call(collect_kernel, out_shape=(shaped(records, P_SIZE),) * 2,...  2.23 us
  transfers between devices with their start and end apart: 3, of which 2 were waited for; matrix products, arithmetic and copies ran while one was open for 0% of the time, Pallas kernels for 0%

profile of v1, /device:TPU:1, one launch (start us, length us, event | category | flops | bytes accessed | tf_op | source)
XLA Modules:
  0.0 55.7 jit_solution(10721537213609993097)
XLA Ops:
  1.3 2.3 %make_requests.1 = (f32[512,128]{1,0:T(8,128)}, f32[8,256]{1,0:T(8,128)}, f32[8,256]{1,0:T(8,128)}, s32[1,256]{1,0:T(1,128)}) custom-call(f32[64,256]{1,0:T(8,128)} %refs_0_.3, f32[2,16]{1,0:T(2,128)} %refs_1_.1, s32[1,1]{1,0:T(1,128)S(6)} %copy.9.refs_2_, s32[8,1,32]{2,1,0:T(1,128)} %bitcast.14, s32[8,32]{1,0:T(8,128)} %bitcast.15, f32[2,8,32]{2,1,0:T(8,128)} %bitcast.13), custom_call_target="tpu_custom_call" | custom-call | tf_op jit(solution)/shard_map/make_requests/pallas_call | solution.py:202
  3.5 0.0 copy-start.4
  3.5 0.0 copy-start.3
  3.5 11.5 %all-to-all-start = ((f32[128,4,128]{2,1,0:T(4,128)}), f32[128,4,128]{2,1,0:T(4,128)S(1)}, u32[]{:S(2)}, u32[]{:S(2)}) async-start(f32[128,4,128]{2,1,0:T(4,128)} %bitcast.12), calls=%async_computation | async-start | bytes 524288 | tf_op jit(solution)/shard_map/all_to_all | solution.py:223
  15.1 0.0 copy-done.4
  15.1 3.4 %collective-permute-start = (f32[8,256]{1,0:T(8,128)S(1)}, f32[8,256]{1,0:T(8,128)S(1)}, u32[]{:S(2)}, u32[]{:S(2)}) collective-permute-start(f32[8,256]{1,0:T(8,128)S(1)} %copy-done.4), channel_id=1, source_target_pairs={{0,8},{8,16},{16,24},{24,32},{32,40},{40,48},{48,56},{56,64},{64,7... | collective-permute-start | bytes 24584 | tf_op jit(solution)/shard_map/ppermute | solution.py:226
  18.5 0.0 copy-done.3
  18.5 1.3 %collective-permute-start.1 = (f32[8,256]{1,0:T(8,128)S(1)}, f32[8,256]{1,0:T(8,128)S(1)}, u32[]{:S(2)}, u32[]{:S(2)}) collective-permute-start(f32[8,256]{1,0:T(8,128)S(1)} %copy-done.3), channel_id=1, source_target_pairs={{8,0},{16,8},{24,16},{32,24},{40,32},{48,40},{56,48},{64,56},{72,6... | collective-permute-start | bytes 24584 | tf_op jit(solution)/shard_map/ppermute | solution.py:227
  19.8 0.0 collective-permute-done.refs_1_
  19.8 0.0 copy-start.1
  19.8 3.5 %collective-permute-done.1.refs_2_ = f32[8,256]{1,0:T(8,128)S(1)} collective-permute-done((f32[8,256]{1,0:T(8,128)S(1)}, f32[8,256]{1,0:T(8,128)S(1)}, u32[]{:S(2)}, u32[]{:S(2)}) %collective-permute-start.1) | collective-permute-done | bytes 8224 | tf_op jit(solution)/shard_map/ppermute | solution.py:227
  23.3 0.0 copy-start.2
  23.3 2.5 %all-to-all-done = f32[128,4,128]{2,1,0:T(4,128)S(1)} async-done(((f32[128,4,128]{2,1,0:T(4,128)}), f32[128,4,128]{2,1,0:T(4,128)S(1)}, u32[]{:S(2)}, u32[]{:S(2)}) %all-to-all-start) | async-done | bytes 262176 | tf_op jit(solution)/shard_map/all_to_all | solution.py:223
  25.8 0.0 copy-start
  25.8 0.0 copy-done.1
  25.8 0.0 copy-done.2
  25.8 0.7 %copy-done = f32[128,4,128]{2,1,0:T(4,128)} copy-done((f32[128,4,128]{2,1,0:T(4,128)}, f32[128,4,128]{2,1,0:T(4,128)S(1)}, u32[]{:S(2)}) %copy-start) | copy-done | bytes 262168
  26.5 4.4 %step_and_sample.1 = (f32[64,256]{1,0:T(8,128)}, f32[1024,128]{1,0:T(8,128)}) custom-call(f32[64,256]{1,0:T(8,128)} %refs_0_.3, f32[8,256]{1,0:T(8,128)} %copy-done.1, f32[8,256]{1,0:T(8,128)} %copy-done.2, f32[512,128]{1,0:T(8,128)} %bitcast.10), custom_call_target="tpu_custom_call" | custom-call | tf_op jit(solution)/shard_map/step_and_sample/pallas_call | solution.py:228
  30.9 22.6 %all_to_all.22 = f32[128,8,128]{2,1,0:T(8,128)} all-to-all(f32[128,8,128]{2,1,0:T(8,128)} %bitcast.11), channel_id=1, replica_groups=mesh['ty'=16,'tx'=8] {'ty','tx'}, dimensions={0} | all-to-all | bytes 1048576 | tf_op jit(solution)/shard_map/all_to_all | solution.py:223
  53.5 2.2 %collect.1 = (f32[256,128]{1,0:T(8,128)}, f32[256,128]{1,0:T(8,128)}) custom-call(s32[1,256]{1,0:T(1,128)} %get-tuple-element.15.slot_ref, f32[1024,128]{1,0:T(8,128)} %bitcast.9), custom_call_target="tpu_custom_call" | custom-call | tf_op jit(solution)/shard_map/collect/pallas_call | solution.py:237
Async XLA Ops:
  3.5 11.5 %copy-start.4 = (f32[8,256]{1,0:T(8,128)S(1)}, f32[8,256]{1,0:T(8,128)}, u32[]{:S(2)}) copy-start(f32[8,256]{1,0:T(8,128)} %get-tuple-element.11) | copy-start | bytes 24580
  3.5 14.9 %copy-start.3 = (f32[8,256]{1,0:T(8,128)S(1)}, f32[8,256]{1,0:T(8,128)}, u32[]{:S(2)}) copy-start(f32[8,256]{1,0:T(8,128)} %get-tuple-element.12) | copy-start | bytes 24580
  3.5 22.3 %all-to-all-start = ((f32[128,4,128]{2,1,0:T(4,128)}), f32[128,4,128]{2,1,0:T(4,128)S(1)}, u32[]{:S(2)}, u32[]{:S(2)}) async-start(f32[128,4,128]{2,1,0:T(4,128)} %bitcast.12), calls=%async_computation | async-start | bytes 524288 | tf_op jit(solution)/shard_map/all_to_all | solution.py:223
  15.1 4.7 %collective-permute-start = (f32[8,256]{1,0:T(8,128)S(1)}, f32[8,256]{1,0:T(8,128)S(1)}, u32[]{:S(2)}, u32[]{:S(2)}) collective-permute-start(f32[8,256]{1,0:T(8,128)S(1)} %copy-done.4), channel_id=1, source_target_pairs={{0,8},{8,16},{16,24},{24,32},{32,40},{40,48},{48,56},{56,64},{64,7... | collective-permute-start | bytes 24584 | tf_op jit(solution)/shard_map/ppermute | solution.py:226
  18.5 4.8 %collective-permute-start.1 = (f32[8,256]{1,0:T(8,128)S(1)}, f32[8,256]{1,0:T(8,128)S(1)}, u32[]{:S(2)}, u32[]{:S(2)}) collective-permute-start(f32[8,256]{1,0:T(8,128)S(1)} %copy-done.3), channel_id=1, source_target_pairs={{8,0},{16,8},{24,16},{32,24},{40,32},{48,40},{56,48},{64,56},{72,6... | collective-permute-start | bytes 24584 | tf_op jit(solution)/shard_map/ppermute | solution.py:227
  19.8 6.0 %copy-start.1 = (f32[8,256]{1,0:T(8,128)}, f32[8,256]{1,0:T(8,128)S(1)}, u32[]{:S(2)}) copy-start(f32[8,256]{1,0:T(8,128)S(1)} %collective-permute-done.refs_1_) | copy-start | bytes 24580
  23.3 2.5 %copy-start.2 = (f32[8,256]{1,0:T(8,128)}, f32[8,256]{1,0:T(8,128)S(1)}, u32[]{:S(2)}) copy-start(f32[8,256]{1,0:T(8,128)S(1)} %collective-permute-done.1.refs_2_) | copy-start | bytes 24580
  25.8 0.7 %copy-start = (f32[128,4,128]{2,1,0:T(4,128)}, f32[128,4,128]{2,1,0:T(4,128)S(1)}, u32[]{:S(2)}) copy-start(f32[128,4,128]{2,1,0:T(4,128)S(1)} %all-to-all-done) | copy-start | bytes 786436

commit v2 on v1

--- a/solution.py
+++ b/solution.py
@@ -18,6 +18,8 @@
 BF16 = jnp.bfloat16
 VMEM = pl.BlockSpec(memory_space=pltpu.VMEM)
 SMEM = pl.BlockSpec(memory_space=pltpu.SMEM)
+HBM = pl.BlockSpec(memory_space=pltpu.HBM)
+PARAMS = pltpu.CompilerParams(vmem_limit_bytes=8 << 20)
 
 
 def iota(shape, dim):
@@ -32,16 +34,22 @@
     return high, middle, low
 
 
-def request_kernel(
-    n_tx, screen_ref, table_ref, index_ref, tile_ref, cell_ref, frac_ref,
-    send_ref, top_ref, bottom_ref, slot_ref,
-):
+def request_kernel(n_tx, index_ref, *refs):
+    sources, refs = refs[:5], refs[5:]
+    (send_ref, edge_ref, slot_ref), refs = refs[:3], refs[3:]
+    copies = [pltpu.make_async_copy(sources[i], refs[i], refs[5].at[i]) for i in range(5)]
+    for copy in copies:
+        copy.start()
+    screen_ref, table_ref, tile_ref, cell_ref, frac_ref = refs[:5]
+    for copy in copies:
+        copy.wait()
     tx = lax.axis_index("tx")
     groups, width = tile_ref.shape[0], tile_ref.shape[2]
     records = groups * width
     tiles = send_ref.shape[0] // SUB
-    top_ref[...] = screen_ref[0:8, :]
-    bottom_ref[...] = screen_ref[RY - 8 : RY, :]
+    edge_ref[...] = jnp.where(
+        iota((2 * SUB, RX), 0) < SUB, screen_ref[0 : 2 * SUB, :], screen_ref[RY - 2 * SUB : RY, :]
+    )
 
     def flat(rows):
         return jnp.concatenate(rows, axis=1)
@@ -74,7 +82,7 @@
     for k in range(1, CAP):
         requests = requests + pltpu.roll(found[k * tiles : (k + 1) * tiles], 4 * k, axis=1)
 
-    chosen = jnp.where(iota((2, table_ref.shape[1]), 1) == index_ref[...], table_ref[...], 0.0)
+    chosen = jnp.where(iota((2, table_ref.shape[1]), 1) == index_ref[0, 0], table_ref[...], 0.0)
     wind = jnp.sum(chosen, axis=1, keepdims=True)
     lane = iota((1, 128), 1)
     winds = jnp.where(lane == REC, wind[0:1], jnp.where(lane == REC + 1, wind[1:2], 0.0))
@@ -95,7 +103,7 @@
 
 
 def sample_kernel(
-    n_ty, n_tx, screen_ref, north_ref, south_ref, got_ref, next_ref, reply_ref, edge_ref
+    n_ty, n_tx, screen_ref, inner_ref, outer_ref, got_ref, next_ref, reply_ref, edge_ref
 ):
     ty, tx = lax.axis_index("ty"), lax.axis_index("tx")
     tiles = n_ty * n_tx
@@ -119,7 +127,8 @@
     sides = edge_ref[...].T[0 : RY + 2 * SUB]
 
     rows, cols = RY + 2 * SUB, RX + 128
-    ends = jnp.where(iota((2 * SUB, RX), 0) < SUB, south_ref[...], north_ref[...])
+    even = lax.rem(ty, 2) == 0
+    ends = jnp.where((iota((2 * SUB, RX), 0) < SUB) == even, inner_ref[...], outer_ref[...])
     field = jnp.concatenate(
         [jnp.concatenate([screen_ref[...], ends], axis=0), sides], axis=1
     )
@@ -199,46 +208,64 @@
     def shaped(*shape, dtype=F32):
         return jax.ShapeDtypeStruct(shape, dtype)
 
-    send, top, bottom, slots = pl.pallas_call(
+    send, edges, slots = pl.pallas_call(
         lambda *refs: request_kernel(n_tx, *refs),
         out_shape=(
             shaped(tiles * SUB, 128),
-            shaped(8, RX),
-            shaped(8, RX),
+            shaped(2 * SUB, RX),
             shaped(1, records, dtype=jnp.int32),
         ),
-        in_specs=[VMEM] * 6,
-        out_specs=(VMEM,) * 4,
+        in_specs=[SMEM] + [HBM] * 5,
+        out_specs=(VMEM,) * 3,
+        scratch_shapes=[
+            pltpu.VMEM((RY, RX), F32),
+            pltpu.VMEM(wind_table.shape, F32),
+            pltpu.VMEM((groups, 1, width), jnp.int32),
+            pltpu.VMEM((groups, width), jnp.int32),
+            pltpu.VMEM((2, groups, width), F32),
+            pltpu.SemaphoreType.DMA((5,)),
+        ],
+        compiler_params=PARAMS,
         name="make_requests",
     )(
-        screen,
-        wind_table,
         wind_index,
-        tile_id.reshape(groups, 1, width),
-        cell_index.reshape(groups, width),
-        fractions.reshape(2, groups, width),
+        *[
+            pltpu.with_memory_space_constraint(x, pltpu.HBM)
+            for x in (
+                screen,
+                wind_table,
+                tile_id.reshape(groups, 1, width),
+                cell_index.reshape(groups, width),
+                fractions.reshape(2, groups, width),
+            )
+        ],
     )
 
     def exchange(x):
         return lax.all_to_all(x, ("ty", "tx"), split_axis=0, concat_axis=0, tiled=True)
 
     got = exchange(send)
-    north = lax.ppermute(bottom, "ty", [(i, i + 1) for i in range(n_ty - 1)])
-    south = lax.ppermute(top, "ty", [(i + 1, i) for i in range(n_ty - 1)])
+    def swap(first):
+        pairs = [(i, i + 1) for i in range(first, n_ty - 1, 2)]
+        return lax.ppermute(edges, "ty", pairs + [(j, i) for i, j in pairs])
+
+    inner, outer = swap(0), swap(1)
     screen_next, reply = pl.pallas_call(
         lambda *refs: sample_kernel(n_ty, n_tx, *refs),
         out_shape=(shaped(RY, RX), shaped(tiles * 2 * CAP, 128)),
         in_specs=[VMEM] * 4,
         out_specs=(VMEM,) * 2,
         scratch_shapes=[pltpu.VMEM((128, 128), F32)],
+        compiler_params=PARAMS,
         name="step_and_sample",
-    )(screen, north, south, got)
+    )(screen, inner, outer, got)
     returned = exchange(reply)
     phases, slopes = pl.pallas_call(
         collect_kernel,
         out_shape=(shaped(records, P_SIZE),) * 2,
         in_specs=[SMEM, VMEM],
         out_specs=(VMEM,) * 2,
+        compiler_params=PARAMS,
         name="collect",
     )(slots, returned)
     out_shape = (1, 1, groups, width, P_SIZE)

time: 56.1 us -> 50.4 us (0.90)
  blocking collectives: 22.6 us -> 20 us
  Pallas kernels: 8.87 us -> 6.56 us
  local copies, waits for them, and re-layouts: 0.71 us -> 0.01 us
    all_to_all x1, blocking collectives: 22.6 us -> 20 us  [exchange(): lax.all_to_all(x, ('ty', 'tx'), split_axis=0, concat_axis=0, tiled=True)]
    ppermute x2, waiting for transfers between devices: 3.51 us -> 1.37 us  [swap(): return lax.ppermute(edges, 'ty', pairs + [(j, i) for i, j in pairs])]
    all_to_all x1, waiting for transfers between devices: 2.51 us -> 4.45 us  [exchange(): lax.all_to_all(x, ('ty', 'tx'), split_axis=0, concat_axis=0, tiled=True)]
    pallas_call x1, Pallas kernels: 4.37 us -> 2.56 us  [local(): pl.pallas_call(lambda *refs: sample_kernel(n_ty, n_tx, *refs), out_shape=...]
    unnamed x10 -> x2, local copies, waits for them, and re-layouts: 0.71 us -> 0.01 us
where the time goes in v2:
time: 50.4 us; the launch traced here: 50.1 us
  blocking collectives  20 us (40%)
  starting transfers between devices  16.4 us (33%)
  Pallas kernels  6.56 us (13%)
  waiting for transfers between devices  5.82 us (12%)
  between operations  1.31 us (3%)
    all_to_all x1, blocking collectives, exchange(): lax.all_to_all(x, ('ty', 'tx'), split_axis=0, concat_axis=0, tiled=True)  20 us
    all_to_all x1, starting transfers between devices, exchange(): lax.all_to_all(x, ('ty', 'tx'), split_axis=0, concat_axis=0, tiled=True)  11.5 us
    ppermute x2, starting transfers between devices, swap(): return lax.ppermute(edges, 'ty', pairs + [(j, i) for i, j in pairs])  4.95 us
    all_to_all x1, waiting for transfers between devices, exchange(): lax.all_to_all(x, ('ty', 'tx'), split_axis=0, concat_axis=0, tiled=True)  4.45 us
    pallas_call x1, Pallas kernels, local(): pl.pallas_call(lambda *refs: sample_kernel(n_ty, n_tx, *refs), out_shape=...  2.56 us
    pallas_call x1, Pallas kernels, local(): pl.pallas_call(lambda *refs: request_kernel(n_tx, *refs), out_shape=(shap...  2.26 us
    pallas_call x1, Pallas kernels, local(): pl.pallas_call(collect_kernel, out_shape=(shaped(records, P_SIZE),) * 2,...  1.73 us
    ppermute x2, waiting for transfers between devices, swap(): return lax.ppermute(edges, 'ty', pairs + [(j, i) for i, j in pairs])  1.37 us
  transfers between devices with their start and end apart: 3, of which 2 were waited for; matrix products, arithmetic and copies ran while one was open for 0% of the time, Pallas kernels for 0%

profile of v2, /device:TPU:1, one launch (start us, length us, event | category | flops | bytes accessed | tf_op | source)
XLA Modules:
  0.0 50.1 jit_solution(16276728043350403388)
XLA Ops:
  1.3 2.3 %make_requests.1 = (f32[512,128]{1,0:T(8,128)}, f32[8,256]{1,0:T(8,128)S(1)}, s32[1,256]{1,0:T(1,128)S(1)}) custom-call(s32[1,1]{1,0:T(1,128)S(6)} %copy.9.refs_0_, f32[64,256]{1,0:T(8,128)} %refs_0_.2, f32[2,16]{1,0:T(2,128)} %refs_2_.1, s32[8,1,32]{2,1,0:T(1,128)} %bitcast.13, s32[8,32]{1,0:T(8,128)} %bitcast.14, f32[2,8,32]{2,1,0:T(8,128)} %bitcast.12), custom_call_target="tpu_custom_call" | custom-call | tf_op jit(solution)/shard_map/make_requests/pallas_call | solution.py:211
  3.5 0.0 copy-start
  3.6 11.5 %all-to-all-start = ((f32[128,4,128]{2,1,0:T(4,128)}), f32[128,4,128]{2,1,0:T(4,128)S(1)}, u32[]{:S(2)}, u32[]{:S(2)}) async-start(f32[128,4,128]{2,1,0:T(4,128)} %bitcast.3), calls=%async_computation | async-start | bytes 524288 | tf_op jit(solution)/shard_map/all_to_all | solution.py:245
  15.1 0.7 %collective-permute-start.1 = (f32[8,256]{1,0:T(8,128)S(1)}, f32[8,256]{1,0:T(8,128)S(1)}, u32[]{:S(2)}, u32[]{:S(2)}) collective-permute-start(f32[8,256]{1,0:T(8,128)S(1)} %get-tuple-element.10), channel_id=1, source_target_pairs={{8,16},{24,32},{40,48},{56,64},{72,80},{88,96},{104,112},{16,8},{3... | collective-permute-start | bytes 24584 | tf_op jit(solution)/shard_map/ppermute | solution.py:250
  15.7 4.3 %collective-permute-start = (f32[8,256]{1,0:T(8,128)S(1)}, f32[8,256]{1,0:T(8,128)S(1)}, u32[]{:S(2)}, u32[]{:S(2)}) collective-permute-start(f32[8,256]{1,0:T(8,128)S(1)} %get-tuple-element.10), channel_id=1, source_target_pairs={{0,8},{16,24},{32,40},{48,56},{64,72},{80,88},{96,104},{112,120},{... | collective-permute-start | bytes 24584 | tf_op jit(solution)/shard_map/ppermute | solution.py:250
  20.0 0.0 collective-permute-done.1.refs_2_
  20.0 1.4 %collective-permute-done.refs_1_ = f32[8,256]{1,0:T(8,128)S(1)} collective-permute-done((f32[8,256]{1,0:T(8,128)S(1)}, f32[8,256]{1,0:T(8,128)S(1)}, u32[]{:S(2)}, u32[]{:S(2)}) %collective-permute-start) | collective-permute-done | bytes 8224 | tf_op jit(solution)/shard_map/ppermute | solution.py:250
  21.4 4.5 %all-to-all-done = f32[128,4,128]{2,1,0:T(4,128)S(1)} async-done(((f32[128,4,128]{2,1,0:T(4,128)}), f32[128,4,128]{2,1,0:T(4,128)S(1)}, u32[]{:S(2)}, u32[]{:S(2)}) %all-to-all-start) | async-done | bytes 262176 | tf_op jit(solution)/shard_map/all_to_all | solution.py:245
  25.8 0.0 copy-done
  25.8 2.6 %step_and_sample.1 = (f32[64,256]{1,0:T(8,128)}, f32[1024,128]{1,0:T(8,128)S(1)}) custom-call(f32[64,256]{1,0:T(8,128)S(1)} %copy-done, f32[8,256]{1,0:T(8,128)S(1)} %collective-permute-done.refs_1_, f32[8,256]{1,0:T(8,128)S(1)} %collective-permute-done.1.refs_2_, f32[512,128]{1,0:T(8,128)S(1)} %bitcast.10), custom_call_target="tpu_custom_call" | custom-call | tf_op jit(solution)/shard_map/step_and_sample/pallas_call | solution.py:253
  28.4 20.0 %all_to_all.22 = f32[128,8,128]{2,1,0:T(8,128)S(1)} all-to-all(f32[128,8,128]{2,1,0:T(8,128)S(1)} %bitcast.11), channel_id=1, replica_groups=mesh['ty'=16,'tx'=8] {'ty','tx'}, dimensions={0} | all-to-all | bytes 1048576 | tf_op jit(solution)/shard_map/all_to_all | solution.py:245
  48.4 1.7 %collect.1 = (f32[256,128]{1,0:T(8,128)}, f32[256,128]{1,0:T(8,128)}) custom-call(s32[1,256]{1,0:T(1,128)S(1)} %get-tuple-element.13.slot_ref, f32[1024,128]{1,0:T(8,128)S(1)} %bitcast.9), custom_call_target="tpu_custom_call" | custom-call | tf_op jit(solution)/shard_map/collect/pallas_call | solution.py:263
Async XLA Ops:
  3.5 22.3 %copy-start = (f32[64,256]{1,0:T(8,128)S(1)}, f32[64,256]{1,0:T(8,128)}, u32[]{:S(2)}) copy-start(f32[64,256]{1,0:T(8,128)} %refs_0_.2) | copy-start | bytes 196612
  3.6 22.3 %all-to-all-start = ((f32[128,4,128]{2,1,0:T(4,128)}), f32[128,4,128]{2,1,0:T(4,128)S(1)}, u32[]{:S(2)}, u32[]{:S(2)}) async-start(f32[128,4,128]{2,1,0:T(4,128)} %bitcast.3), calls=%async_computation | async-start | bytes 524288 | tf_op jit(solution)/shard_map/all_to_all | solution.py:245
  15.1 5.0 %collective-permute-start.1 = (f32[8,256]{1,0:T(8,128)S(1)}, f32[8,256]{1,0:T(8,128)S(1)}, u32[]{:S(2)}, u32[]{:S(2)}) collective-permute-start(f32[8,256]{1,0:T(8,128)S(1)} %get-tuple-element.10), channel_id=1, source_target_pairs={{8,16},{24,32},{40,48},{56,64},{72,80},{88,96},{104,112},{16,8},{3... | collective-permute-start | bytes 24584 | tf_op jit(solution)/shard_map/ppermute | solution.py:250
  15.7 5.7 %collective-permute-start = (f32[8,256]{1,0:T(8,128)S(1)}, f32[8,256]{1,0:T(8,128)S(1)}, u32[]{:S(2)}, u32[]{:S(2)}) collective-permute-start(f32[8,256]{1,0:T(8,128)S(1)} %get-tuple-element.10), channel_id=1, source_target_pairs={{0,8},{16,24},{32,40},{48,56},{64,72},{80,88},{96,104},{112,120},{... | collective-permute-start | bytes 24584 | tf_op jit(solution)/shard_map/ppermute | solution.py:250

commit v3 on v2

--- a/solution.py
+++ b/solution.py
@@ -12,6 +12,8 @@
 SUB = 4
 CAP = 4
 DIFFUSION = 0.2
+PARTS = 2
+UNROLL = 32
 
 REC = 64
 F32 = jnp.float32
@@ -36,20 +38,19 @@
 
 def request_kernel(n_tx, index_ref, *refs):
     sources, refs = refs[:5], refs[5:]
-    (send_ref, edge_ref, slot_ref), refs = refs[:3], refs[3:]
+    (send_ref, edge_ref, slot_out), refs = refs[:3], refs[3:]
+    (slot_ref, slot_sem), refs = refs[:2], refs[2:]
     copies = [pltpu.make_async_copy(sources[i], refs[i], refs[5].at[i]) for i in range(5)]
     for copy in copies:
         copy.start()
     screen_ref, table_ref, tile_ref, cell_ref, frac_ref = refs[:5]
-    for copy in copies:
-        copy.wait()
     tx = lax.axis_index("tx")
     groups, width = tile_ref.shape[0], tile_ref.shape[2]
     records = groups * width
     tiles = send_ref.shape[0] // SUB
-    edge_ref[...] = jnp.where(
-        iota((2 * SUB, RX), 0) < SUB, screen_ref[0 : 2 * SUB, :], screen_ref[RY - 2 * SUB : RY, :]
-    )
+    before = (iota((records, records), 0) < iota((records, records), 1)).astype(F32).astype(BF16)
+    for copy in copies[2:]:
+        copy.wait()
 
     def flat(rows):
         return jnp.concatenate(rows, axis=1)
@@ -60,10 +61,11 @@
     frac_col = flat([frac_ref[1, s : s + 1, :] for s in range(groups)])
 
     names = jnp.where(iota((tiles, records), 0) == tile, 1.0, 0.0)
-    before = (iota((records, records), 0) < iota((records, records), 1)).astype(F32).astype(BF16)
     earlier = jnp.dot(names.astype(BF16), before, preferred_element_type=F32)
     rank = jnp.sum(names * earlier, axis=0, keepdims=True)
     slot_ref[...] = tile * (2 * CAP) + 2 * rank.astype(jnp.int32)
+    slots = pltpu.make_async_copy(slot_ref, slot_out, slot_sem)
+    slots.start()
 
     picks = jnp.concatenate(
         [jnp.where(earlier == k, names, 0.0).astype(BF16) for k in range(CAP)], axis=0
@@ -82,6 +84,11 @@
     for k in range(1, CAP):
         requests = requests + pltpu.roll(found[k * tiles : (k + 1) * tiles], 4 * k, axis=1)
 
+    for copy in copies[:2]:
+        copy.wait()
+    edge_ref[...] = jnp.where(
+        iota((2 * SUB, RX), 0) < SUB, screen_ref[0 : 2 * SUB, :], screen_ref[RY - 2 * SUB : RY, :]
+    )
     chosen = jnp.where(iota((2, table_ref.shape[1]), 1) == index_ref[0, 0], table_ref[...], 0.0)
     wind = jnp.sum(chosen, axis=1, keepdims=True)
     lane = iota((1, 128), 1)
@@ -100,10 +107,11 @@
         if c == 1:
             row = row + winds
         send_ref[pl.ds(c, tiles, stride=SUB), :] = row
+    slots.wait()
 
 
 def sample_kernel(
-    n_ty, n_tx, screen_ref, inner_ref, outer_ref, got_ref, next_ref, reply_ref, edge_ref
+    n_ty, n_tx, screen_ref, inner_ref, outer_ref, got_ref, next_ref, reply_ref, edge_ref, tile_ref, sem
 ):
     ty, tx = lax.axis_index("ty"), lax.axis_index("tx")
     tiles = n_ty * n_tx
@@ -158,45 +166,66 @@
         spread = east + west + south + north - 4.0 * field
         field = jnp.where(inside, field - 0.5 * advect + DIFFUSION * spread, 0.0)
     tile = field[0:RY, 0:RX]
-    next_ref[...] = tile
-
-    parts = jnp.concatenate(three_terms(tile), axis=0)
+    tile_ref[...] = tile
+    store = pltpu.make_async_copy(tile_ref, next_ref, sem)
+    store.start()
+
+    both = jnp.concatenate([tile, pltpu.roll(tile, RX - 1, axis=1)], axis=1)
+    parts = jnp.concatenate(three_terms(both), axis=0)
     records = got_ref[pl.ds(0, tiles, stride=SUB), :]
-    start_row = jnp.floor((records + 0.5) * (1.0 / SPAN))
-    start_col = (records - SPAN * start_row).astype(jnp.int32)
     line = lax.rem(iota((tiles, 3 * RY), 1), RY).astype(F32)
     lanes = iota((tiles, 128), 1)
     for k in range(CAP):
         at = REC + 4 * k
-        row_k, col_k = start_row[:, at : at + 1], start_col[:, at : at + 1]
-        frac_row, frac_col = records[:, at + 1 : at + 2], records[:, at + 2 : at + 3]
-        upper = jnp.dot(
-            jnp.where(line == row_k, 1.0, 0.0).astype(BF16), parts, preferred_element_type=F32
-        )
-        lower = jnp.dot(
-            jnp.where(line == row_k + 1.0, 1.0, 0.0).astype(BF16), parts, preferred_element_type=F32
-        )
-        spot = lanes + col_k
-        near = spot < 128
-        spot = spot & 127
-        for p, value in enumerate(((1.0 - frac_row) * upper + frac_row * lower, lower - upper)):
-            value = (1.0 - frac_col) * value + frac_col * pltpu.roll(value, RX - 1, axis=1)
-            strip = jnp.where(
-                near,
-                jnp.take_along_axis(value[:, 0:128], spot, axis=1),
-                jnp.take_along_axis(value[:, 128:256], spot, axis=1),
+        cell, frac_row, frac_col = [records[:, at + v : at + v + 1] for v in range(3)]
+        cell = jnp.broadcast_to(cell, (tiles, 128))
+        row_k = jnp.floor((cell + 0.5) * (1.0 / SPAN))
+        col_k = (cell - SPAN * row_k).astype(jnp.int32)
+        row_k = jnp.concatenate([row_k, row_k[:, 0 : 3 * RY - 128]], axis=1)
+        upper, lower = [
+            jnp.dot(
+                jnp.where(line == row_k + d, 1.0, 0.0).astype(BF16), parts, preferred_element_type=F32
             )
-            reply_ref[pl.ds(2 * k + p, tiles, stride=2 * CAP), :] = strip
-
-
-def collect_kernel(slot_ref, got_ref, phase_ref, slope_ref):
-    def step(n, carry):
-        slot = slot_ref[0, n]
-        phase_ref[pl.ds(n, 1), :] = got_ref[pl.ds(slot, 1), :]
-        slope_ref[pl.ds(n, 1), :] = got_ref[pl.ds(slot + 1, 1), :]
-        return carry
-
-    lax.fori_loop(0, phase_ref.shape[0], step, 0, unroll=8)
+            for d in (0.0, 1.0)
+        ]
+        far = lanes < col_k
+        spot = (lanes + col_k) & 127
+        upper, lower = [
+            [
+                jnp.where(far, value[:, at + 128 : at + 256], value[:, at : at + 128])
+                for at in (0, RX)
+            ]
+            for value in (upper, lower)
+        ]
+        rows = [(1.0 - frac_row) * upper[i] + frac_row * lower[i] for i in range(2)]
+        steps = [lower[i] - upper[i] for i in range(2)]
+        for p, (left, right) in enumerate((rows, steps)):
+            value = (1.0 - frac_col) * left + frac_col * right
+            reply_ref[pl.ds(2 * k + p, tiles, stride=2 * CAP), :] = jnp.take_along_axis(
+                value, spot, axis=1
+            )
+    store.wait()
+
+
+def collect_kernel(slot_ref, got_ref, phase_ref, slope_ref, phase_rows, slope_rows, sems):
+    records = phase_rows.shape[0]
+    part = records // PARTS
+    stores = []
+    for p in range(PARTS):
+
+        def step(n, carry):
+            slot = slot_ref[0, n]
+            phase_rows[pl.ds(n, 1), :] = got_ref[pl.ds(slot, 1), :]
+            slope_rows[pl.ds(n, 1), :] = got_ref[pl.ds(slot + 1, 1), :]
+            return carry
+
+        lax.fori_loop(p * part, (p + 1) * part, step, 0, unroll=UNROLL)
+        for i, (rows, out) in enumerate(((phase_rows, phase_ref), (slope_rows, slope_ref))):
+            here = pl.ds(p * part, part)
+            stores.append(pltpu.make_async_copy(rows.at[here], out.at[here], sems.at[2 * p + i]))
+            stores[-1].start()
+    for store in stores:
+        store.wait()
 
 
 def local(screen, wind_table, wind_index, tile_id, cell_index, fractions):
@@ -213,11 +242,13 @@
         out_shape=(
             shaped(tiles * SUB, 128),
             shaped(2 * SUB, RX),
-            shaped(1, records, dtype=jnp.int32),
+            pltpu.SMEM((1, records), jnp.int32),
         ),
         in_specs=[SMEM] + [HBM] * 5,
-        out_specs=(VMEM,) * 3,
+        out_specs=(VMEM, VMEM, SMEM),
         scratch_shapes=[
+            pltpu.VMEM((1, records), jnp.int32),
+            pltpu.SemaphoreType.DMA,
             pltpu.VMEM((RY, RX), F32),
             pltpu.VMEM(wind_table.shape, F32),
             pltpu.VMEM((groups, 1, width), jnp.int32),
@@ -254,8 +285,12 @@
         lambda *refs: sample_kernel(n_ty, n_tx, *refs),
         out_shape=(shaped(RY, RX), shaped(tiles * 2 * CAP, 128)),
         in_specs=[VMEM] * 4,
-        out_specs=(VMEM,) * 2,
-        scratch_shapes=[pltpu.VMEM((128, 128), F32)],
+        out_specs=(HBM, VMEM),
+        scratch_shapes=[
+            pltpu.VMEM((128, 128), F32),
+            pltpu.VMEM((RY, RX), F32),
+            pltpu.SemaphoreType.DMA,
+        ],
         compiler_params=PARAMS,
         name="step_and_sample",
     )(screen, inner, outer, got)
@@ -264,7 +299,12 @@
         collect_kernel,
         out_shape=(shaped(records, P_SIZE),) * 2,
         in_specs=[SMEM, VMEM],
-        out_specs=(VMEM,) * 2,
+        out_specs=(HBM,) * 2,
+        scratch_shapes=[
+            pltpu.VMEM((records, P_SIZE), F32),
+            pltpu.VMEM((records, P_SIZE), F32),
+            pltpu.SemaphoreType.DMA((2 * PARTS,)),
+        ],
         compiler_params=PARAMS,
         name="collect",
     )(slots, returned)

time: 50.4 us -> 48.5 us (0.962)
  Pallas kernels: 6.56 us -> 4.63 us
    pallas_call x1, Pallas kernels: 2.56 us -> 1.33 us  [local(): pl.pallas_call(lambda *refs: sample_kernel(n_ty, n_tx, *refs), out_shape=...]
    pallas_call x1, Pallas kernels: 1.73 us -> 0.96 us  [local(): pl.pallas_call(collect_kernel, out_shape=(shaped(records, P_SIZE),) * 2,...]
where the time goes in v3:
time: 48.5 us; the launch traced here: 48.2 us
  blocking collectives  20 us (41%)
  starting transfers between devices  16.4 us (34%)
  waiting for transfers between devices  5.82 us (12%)
  Pallas kernels  4.63 us (10%)
  between operations  1.32 us (3%)
    all_to_all x1, blocking collectives, exchange(): lax.all_to_all(x, ('ty', 'tx'), split_axis=0, concat_axis=0, tiled=True)  20 us
    all_to_all x1, starting transfers between devices, exchange(): lax.all_to_all(x, ('ty', 'tx'), split_axis=0, concat_axis=0, tiled=True)  11.5 us
    ppermute x2, starting transfers between devices, swap(): return lax.ppermute(edges, 'ty', pairs + [(j, i) for i, j in pairs])  4.95 us
    all_to_all x1, waiting for transfers between devices, exchange(): lax.all_to_all(x, ('ty', 'tx'), split_axis=0, concat_axis=0, tiled=True)  4.45 us
    pallas_call x1, Pallas kernels, local(): pl.pallas_call(lambda *refs: request_kernel(n_tx, *refs), out_shape=(shap...  2.34 us
    ppermute x2, waiting for transfers between devices, swap(): return lax.ppermute(edges, 'ty', pairs + [(j, i) for i, j in pairs])  1.37 us
    pallas_call x1, Pallas kernels, local(): pl.pallas_call(lambda *refs: sample_kernel(n_ty, n_tx, *refs), out_shape=...  1.33 us
  transfers between devices with their start and end apart: 3, of which 2 were waited for; matrix products, arithmetic and copies ran while one was open for 0% of the time, Pallas kernels for 0%

profile of v3, /device:TPU:1, one launch (start us, length us, event | category | flops | bytes accessed | tf_op | source)
XLA Modules:
  0.0 48.2 jit_solution(15781254383850856504)
XLA Ops:
  1.3 2.3 %make_requests.1 = (f32[512,128]{1,0:T(8,128)}, f32[8,256]{1,0:T(8,128)S(1)}, s32[1,256]{1,0:T(1,128)S(4)}) custom-call(s32[1,1]{1,0:T(1,128)S(6)} %copy.9.refs_0_, f32[64,256]{1,0:T(8,128)} %refs_0_.2, f32[2,16]{1,0:T(2,128)} %refs_2_.1, s32[8,1,32]{2,1,0:T(1,128)} %bitcast.13, s32[8,32]{1,0:T(8,128)} %bitcast.14, f32[2,8,32]{2,1,0:T(8,128)} %bitcast.12), custom_call_target="tpu_custom_call" | custom-call | tf_op jit(solution)/shard_map/make_requests/pallas_call | solution.py:240
  3.6 0.0 copy-start
  3.6 11.5 %all-to-all-start = ((f32[128,4,128]{2,1,0:T(4,128)}), f32[128,4,128]{2,1,0:T(4,128)S(1)}, u32[]{:S(2)}, u32[]{:S(2)}) async-start(f32[128,4,128]{2,1,0:T(4,128)} %bitcast.3), calls=%async_computation | async-start | bytes 524288 | tf_op jit(solution)/shard_map/all_to_all | solution.py:276
  15.1 0.7 %collective-permute-start.1 = (f32[8,256]{1,0:T(8,128)S(1)}, f32[8,256]{1,0:T(8,128)S(1)}, u32[]{:S(2)}, u32[]{:S(2)}) collective-permute-start(f32[8,256]{1,0:T(8,128)S(1)} %get-tuple-element.10), channel_id=1, source_target_pairs={{8,16},{24,32},{40,48},{56,64},{72,80},{88,96},{104,112},{16,8},{3... | collective-permute-start | bytes 24584 | tf_op jit(solution)/shard_map/ppermute | solution.py:281
  15.8 4.3 %collective-permute-start = (f32[8,256]{1,0:T(8,128)S(1)}, f32[8,256]{1,0:T(8,128)S(1)}, u32[]{:S(2)}, u32[]{:S(2)}) collective-permute-start(f32[8,256]{1,0:T(8,128)S(1)} %get-tuple-element.10), channel_id=1, source_target_pairs={{0,8},{16,24},{32,40},{48,56},{64,72},{80,88},{96,104},{112,120},{... | collective-permute-start | bytes 24584 | tf_op jit(solution)/shard_map/ppermute | solution.py:281
  20.1 0.0 collective-permute-done.1.refs_2_
  20.1 1.4 %collective-permute-done.refs_1_ = f32[8,256]{1,0:T(8,128)S(1)} collective-permute-done((f32[8,256]{1,0:T(8,128)S(1)}, f32[8,256]{1,0:T(8,128)S(1)}, u32[]{:S(2)}, u32[]{:S(2)}) %collective-permute-start) | collective-permute-done | bytes 8224 | tf_op jit(solution)/shard_map/ppermute | solution.py:281
  21.5 4.5 %all-to-all-done = f32[128,4,128]{2,1,0:T(4,128)S(1)} async-done(((f32[128,4,128]{2,1,0:T(4,128)}), f32[128,4,128]{2,1,0:T(4,128)S(1)}, u32[]{:S(2)}, u32[]{:S(2)}) %all-to-all-start) | async-done | bytes 262176 | tf_op jit(solution)/shard_map/all_to_all | solution.py:276
  25.9 0.0 copy-done
  25.9 1.3 %step_and_sample.1 = (f32[64,256]{1,0:T(8,128)}, f32[1024,128]{1,0:T(8,128)S(1)}) custom-call(f32[64,256]{1,0:T(8,128)S(1)} %copy-done, f32[8,256]{1,0:T(8,128)S(1)} %collective-permute-done.refs_1_, f32[8,256]{1,0:T(8,128)S(1)} %collective-permute-done.1.refs_2_, f32[512,128]{1,0:T(8,128)S(1)} %bitcast.10), custom_call_target="tpu_custom_call" | custom-call | tf_op jit(solution)/shard_map/step_and_sample/pallas_call | solution.py:284
  27.3 20.0 %all_to_all.22 = f32[128,8,128]{2,1,0:T(8,128)S(1)} all-to-all(f32[128,8,128]{2,1,0:T(8,128)S(1)} %bitcast.11), channel_id=1, replica_groups=mesh['ty'=16,'tx'=8] {'ty','tx'}, dimensions={0} | all-to-all | bytes 1048576 | tf_op jit(solution)/shard_map/all_to_all | solution.py:276
  47.2 1.0 %collect.1 = (f32[256,128]{1,0:T(8,128)}, f32[256,128]{1,0:T(8,128)}) custom-call(s32[1,256]{1,0:T(1,128)S(4)} %get-tuple-element.13.slot_ref, f32[1024,128]{1,0:T(8,128)S(1)} %bitcast.9), custom_call_target="tpu_custom_call" | custom-call | tf_op jit(solution)/shard_map/collect/pallas_call | solution.py:298
Async XLA Ops:
  3.6 22.3 %copy-start = (f32[64,256]{1,0:T(8,128)S(1)}, f32[64,256]{1,0:T(8,128)}, u32[]{:S(2)}) copy-start(f32[64,256]{1,0:T(8,128)} %refs_0_.2) | copy-start | bytes 196612
  3.6 22.3 %all-to-all-start = ((f32[128,4,128]{2,1,0:T(4,128)}), f32[128,4,128]{2,1,0:T(4,128)S(1)}, u32[]{:S(2)}, u32[]{:S(2)}) async-start(f32[128,4,128]{2,1,0:T(4,128)} %bitcast.3), calls=%async_computation | async-start | bytes 524288 | tf_op jit(solution)/shard_map/all_to_all | solution.py:276
  15.1 5.0 %collective-permute-start.1 = (f32[8,256]{1,0:T(8,128)S(1)}, f32[8,256]{1,0:T(8,128)S(1)}, u32[]{:S(2)}, u32[]{:S(2)}) collective-permute-start(f32[8,256]{1,0:T(8,128)S(1)} %get-tuple-element.10), channel_id=1, source_target_pairs={{8,16},{24,32},{40,48},{56,64},{72,80},{88,96},{104,112},{16,8},{3... | collective-permute-start | bytes 24584 | tf_op jit(solution)/shard_map/ppermute | solution.py:281
  15.8 5.7 %collective-permute-start = (f32[8,256]{1,0:T(8,128)S(1)}, f32[8,256]{1,0:T(8,128)S(1)}, u32[]{:S(2)}, u32[]{:S(2)}) collective-permute-start(f32[8,256]{1,0:T(8,128)S(1)} %get-tuple-element.10), channel_id=1, source_target_pairs={{0,8},{16,24},{32,40},{48,56},{64,72},{80,88},{96,104},{112,120},{... | collective-permute-start | bytes 24584 | tf_op jit(solution)/shard_map/ppermute | solution.py:281

commit v4 on v3

--- a/solution.py
+++ b/solution.py
@@ -36,30 +36,24 @@
     return high, middle, low
 
 
-def request_kernel(n_tx, index_ref, *refs):
-    sources, refs = refs[:5], refs[5:]
+def request_kernel(n_tx, index_ref, tile_ref, *refs):
+    sources, refs = refs[:4], refs[4:]
     (send_ref, edge_ref, slot_out), refs = refs[:3], refs[3:]
     (slot_ref, slot_sem), refs = refs[:2], refs[2:]
-    copies = [pltpu.make_async_copy(sources[i], refs[i], refs[5].at[i]) for i in range(5)]
+    copies = [pltpu.make_async_copy(sources[i], refs[i], refs[4].at[i]) for i in range(4)]
     for copy in copies:
         copy.start()
-    screen_ref, table_ref, tile_ref, cell_ref, frac_ref = refs[:5]
+    screen_ref, table_ref, cell_ref, frac_ref = refs[:4]
     tx = lax.axis_index("tx")
     groups, width = tile_ref.shape[0], tile_ref.shape[2]
     records = groups * width
     tiles = send_ref.shape[0] // SUB
     before = (iota((records, records), 0) < iota((records, records), 1)).astype(F32).astype(BF16)
-    for copy in copies[2:]:
-        copy.wait()
 
     def flat(rows):
         return jnp.concatenate(rows, axis=1)
 
     tile = flat([tile_ref[s] for s in range(groups)])
-    cell = flat([cell_ref[s : s + 1, :] for s in range(groups)]).astype(F32)
-    frac_row = flat([frac_ref[0, s : s + 1, :] for s in range(groups)])
-    frac_col = flat([frac_ref[1, s : s + 1, :] for s in range(groups)])
-
     names = jnp.where(iota((tiles, records), 0) == tile, 1.0, 0.0)
     earlier = jnp.dot(names.astype(BF16), before, preferred_element_type=F32)
     rank = jnp.sum(names * earlier, axis=0, keepdims=True)
@@ -70,6 +64,11 @@
     picks = jnp.concatenate(
         [jnp.where(earlier == k, names, 0.0).astype(BF16) for k in range(CAP)], axis=0
     )
+    for copy in copies[2:]:
+        copy.wait()
+    cell = flat([cell_ref[s : s + 1, :] for s in range(groups)]).astype(F32)
+    frac_row = flat([frac_ref[0, s : s + 1, :] for s in range(groups)])
+    frac_col = flat([frac_ref[1, s : s + 1, :] for s in range(groups)])
     line = iota((128, records), 0)
     values = jnp.where(
         line == REC,
@@ -135,8 +134,7 @@
     sides = edge_ref[...].T[0 : RY + 2 * SUB]
 
     rows, cols = RY + 2 * SUB, RX + 128
-    even = lax.rem(ty, 2) == 0
-    ends = jnp.where((iota((2 * SUB, RX), 0) < SUB) == even, inner_ref[...], outer_ref[...])
+    ends = jnp.where((iota((2 * SUB, RX), 0) < SUB) , inner_ref[...], outer_ref[...])
     field = jnp.concatenate(
         [jnp.concatenate([screen_ref[...], ends], axis=0), sides], axis=1
     )
@@ -244,28 +242,27 @@
             shaped(2 * SUB, RX),
             pltpu.SMEM((1, records), jnp.int32),
         ),
-        in_specs=[SMEM] + [HBM] * 5,
+        in_specs=[SMEM, VMEM] + [HBM] * 4,
         out_specs=(VMEM, VMEM, SMEM),
         scratch_shapes=[
             pltpu.VMEM((1, records), jnp.int32),
             pltpu.SemaphoreType.DMA,
             pltpu.VMEM((RY, RX), F32),
             pltpu.VMEM(wind_table.shape, F32),
-            pltpu.VMEM((groups, 1, width), jnp.int32),
             pltpu.VMEM((groups, width), jnp.int32),
             pltpu.VMEM((2, groups, width), F32),
-            pltpu.SemaphoreType.DMA((5,)),
+            pltpu.SemaphoreType.DMA((4,)),
         ],
         compiler_params=PARAMS,
         name="make_requests",
     )(
         wind_index,
+        tile_id.reshape(groups, 1, width),
         *[
             pltpu.with_memory_space_constraint(x, pltpu.HBM)
             for x in (
                 screen,
                 wind_table,
-                tile_id.reshape(groups, 1, width),
                 cell_index.reshape(groups, width),
                 fractions.reshape(2, groups, width),
             )
@@ -276,11 +273,8 @@
         return lax.all_to_all(x, ("ty", "tx"), split_axis=0, concat_axis=0, tiled=True)
 
     got = exchange(send)
-    def swap(first):
-        pairs = [(i, i + 1) for i in range(first, n_ty - 1, 2)]
-        return lax.ppermute(edges, "ty", pairs + [(j, i) for i, j in pairs])
-
-    inner, outer = swap(0), swap(1)
+    north = lax.ppermute(edges, "ty", [(i, (i + 1) % n_ty) for i in range(n_ty)])
+    south = lax.ppermute(edges, "ty", [((i + 1) % n_ty, i) for i in range(n_ty)])
     screen_next, reply = pl.pallas_call(
         lambda *refs: sample_kernel(n_ty, n_tx, *refs),
         out_shape=(shaped(RY, RX), shaped(tiles * 2 * CAP, 128)),
@@ -293,7 +287,7 @@
         ],
         compiler_params=PARAMS,
         name="step_and_sample",
-    )(screen, inner, outer, got)
+    )(screen, south, north, got)
     returned = exchange(reply)
     phases, slopes = pl.pallas_call(
         collect_kernel,

time: 48.5 us -> 47.5 us (0.979)
  blocking collectives: 20 us -> 19 us
  starting transfers between devices: 16.4 us -> 17.1 us
    all_to_all x1, waiting for transfers between devices: 4.45 us -> 2.69 us  [exchange(): lax.all_to_all(x, ('ty', 'tx'), split_axis=0, concat_axis=0, tiled=True)]
    ppermute x2, waiting for transfers between devices: 1.37 us -> 2.66 us  [the longest x1 2.65 us: local(): lax.ppermute(edges, 'ty', [(i, (i + 1) % n_ty) for i in range(n_ty)])]
    all_to_all x1, blocking collectives: 20 us -> 19 us  [exchange(): lax.all_to_all(x, ('ty', 'tx'), split_axis=0, concat_axis=0, tiled=True)]
    ppermute x2, starting transfers between devices: 4.95 us -> 5.57 us  [the longest x1 3.99 us: local(): lax.ppermute(edges, 'ty', [((i + 1) % n_ty, i) for i in range(n_ty)])]
where the time goes in v4:
time: 47.5 us; the launch traced here: 47.3 us
  blocking collectives  19 us (40%)
  starting transfers between devices  17.1 us (36%)
  waiting for transfers between devices  5.34 us (11%)
  Pallas kernels  4.48 us (9%)
  between operations  1.33 us (3%)
    all_to_all x1, blocking collectives, exchange(): lax.all_to_all(x, ('ty', 'tx'), split_axis=0, concat_axis=0, tiled=True)  19 us
    all_to_all x1, starting transfers between devices, exchange(): lax.all_to_all(x, ('ty', 'tx'), split_axis=0, concat_axis=0, tiled=True)  11.5 us
    ppermute x1, starting transfers between devices, local(): lax.ppermute(edges, 'ty', [((i + 1) % n_ty, i) for i in range(n_ty)])  3.99 us
    all_to_all x1, waiting for transfers between devices, exchange(): lax.all_to_all(x, ('ty', 'tx'), split_axis=0, concat_axis=0, tiled=True)  2.69 us
    ppermute x1, waiting for transfers between devices, local(): lax.ppermute(edges, 'ty', [(i, (i + 1) % n_ty) for i in range(n_ty)])  2.65 us
    pallas_call x1, Pallas kernels, local(): pl.pallas_call(lambda *refs: request_kernel(n_tx, *refs), out_shape=(shap...  2.19 us
    ppermute x1, starting transfers between devices, local(): lax.ppermute(edges, 'ty', [(i, (i + 1) % n_ty) for i in range(n_ty)])  1.58 us
    pallas_call x1, Pallas kernels, local(): pl.pallas_call(lambda *refs: sample_kernel(n_ty, n_tx, *refs), out_shape=...  1.33 us
  transfers between devices with their start and end apart: 3, of which 2 were waited for; matrix products, arithmetic and copies ran while one was open for 0% of the time, Pallas kernels for 0%

profile of v4, /device:TPU:1, one launch (start us, length us, event | category | flops | bytes accessed | tf_op | source)
XLA Modules:
  0.0 47.3 jit_solution(12692963693446960496)
XLA Ops:
  0.6 0.0 copy-start.1
  1.3 0.0 copy-done.1
  1.3 2.2 %make_requests.1 = (f32[512,128]{1,0:T(8,128)}, f32[8,256]{1,0:T(8,128)S(1)}, s32[1,256]{1,0:T(1,128)S(4)}) custom-call(s32[1,1]{1,0:T(1,128)S(6)} %copy.9.refs_0_, s32[8,1,32]{2,1,0:T(1,128)S(1)} %bitcast.12, f32[64,256]{1,0:T(8,128)} %refs_0_.2, f32[2,16]{1,0:T(2,128)} %refs_3_.1, s32[8,32]{1,0:T(8,128)} %bitcast.14, f32[2,8,32]{2,1,0:T(8,128)} %bitcast.13), custom_call_target="tpu_custom_call" | custom-call | tf_op jit(solution)/shard_map/make_requests/pallas_call | solution.py:238
  3.5 0.0 copy-start
  3.5 11.5 %all-to-all-start = ((f32[128,4,128]{2,1,0:T(4,128)}), f32[128,4,128]{2,1,0:T(4,128)S(1)}, u32[]{:S(2)}, u32[]{:S(2)}) async-start(f32[128,4,128]{2,1,0:T(4,128)} %bitcast.3), calls=%async_computation | async-start | bytes 524288 | tf_op jit(solution)/shard_map/all_to_all | solution.py:273
  15.0 1.6 %collective-permute-start.1 = (f32[8,256]{1,0:T(8,128)S(1)}, f32[8,256]{1,0:T(8,128)S(1)}, u32[]{:S(2)}, u32[]{:S(2)}) collective-permute-start(f32[8,256]{1,0:T(8,128)S(1)} %get-tuple-element.10), channel_id=1, source_target_pairs={{0,8},{8,16},{16,24},{24,32},{32,40},{40,48},{48,56},{56,64},{64,7... | collective-permute-start | bytes 24584 | tf_op jit(solution)/shard_map/ppermute | solution.py:276
  16.6 4.0 %collective-permute-start = (f32[8,256]{1,0:T(8,128)S(1)}, f32[8,256]{1,0:T(8,128)S(1)}, u32[]{:S(2)}, u32[]{:S(2)}) collective-permute-start(f32[8,256]{1,0:T(8,128)S(1)} %get-tuple-element.10), channel_id=1, source_target_pairs={{8,0},{16,8},{24,16},{32,24},{40,32},{48,40},{56,48},{64,56},{72,6... | collective-permute-start | bytes 24584 | tf_op jit(solution)/shard_map/ppermute | solution.py:277
  20.6 2.7 %collective-permute-done.1.refs_2_ = f32[8,256]{1,0:T(8,128)S(1)} collective-permute-done((f32[8,256]{1,0:T(8,128)S(1)}, f32[8,256]{1,0:T(8,128)S(1)}, u32[]{:S(2)}, u32[]{:S(2)}) %collective-permute-start.1) | collective-permute-done | bytes 8224 | tf_op jit(solution)/shard_map/ppermute | solution.py:276
  23.3 0.0 collective-permute-done.refs_1_
  23.3 2.7 %all-to-all-done = f32[128,4,128]{2,1,0:T(4,128)S(1)} async-done(((f32[128,4,128]{2,1,0:T(4,128)}), f32[128,4,128]{2,1,0:T(4,128)S(1)}, u32[]{:S(2)}, u32[]{:S(2)}) %all-to-all-start) | async-done | bytes 262176 | tf_op jit(solution)/shard_map/all_to_all | solution.py:273
  25.9 0.0 copy-done
  25.9 1.3 %step_and_sample.1 = (f32[64,256]{1,0:T(8,128)}, f32[1024,128]{1,0:T(8,128)S(1)}) custom-call(f32[64,256]{1,0:T(8,128)S(1)} %copy-done, f32[8,256]{1,0:T(8,128)S(1)} %collective-permute-done.refs_1_, f32[8,256]{1,0:T(8,128)S(1)} %collective-permute-done.1.refs_2_, f32[512,128]{1,0:T(8,128)S(1)} %bitcast.10), custom_call_target="tpu_custom_call" | custom-call | tf_op jit(solution)/shard_map/step_and_sample/pallas_call | solution.py:278
  27.3 19.0 %all_to_all.22 = f32[128,8,128]{2,1,0:T(8,128)S(1)} all-to-all(f32[128,8,128]{2,1,0:T(8,128)S(1)} %bitcast.11), channel_id=1, replica_groups=mesh['ty'=16,'tx'=8] {'ty','tx'}, dimensions={0} | all-to-all | bytes 1048576 | tf_op jit(solution)/shard_map/all_to_all | solution.py:273
  46.3 1.0 %collect.1 = (f32[256,128]{1,0:T(8,128)}, f32[256,128]{1,0:T(8,128)}) custom-call(s32[1,256]{1,0:T(1,128)S(4)} %get-tuple-element.13.slot_ref, f32[1024,128]{1,0:T(8,128)S(1)} %bitcast.9), custom_call_target="tpu_custom_call" | custom-call | tf_op jit(solution)/shard_map/collect/pallas_call | solution.py:292
Async XLA Ops:
  0.6 0.7 %copy-start.1 = (s32[1,1,8,32,1]{3,4,2,1,0:T(1,128)S(1)}, s32[1,1,8,32,1]{3,4,2,1,0:T(1,128)}, u32[]{:S(2)}) copy-start(s32[1,1,8,32,1]{3,4,2,1,0:T(1,128)} %param.9) | copy-start | bytes 3076
  3.5 22.4 %copy-start = (f32[64,256]{1,0:T(8,128)S(1)}, f32[64,256]{1,0:T(8,128)}, u32[]{:S(2)}) copy-start(f32[64,256]{1,0:T(8,128)} %refs_0_.2) | copy-start | bytes 196612
  3.5 22.4 %all-to-all-start = ((f32[128,4,128]{2,1,0:T(4,128)}), f32[128,4,128]{2,1,0:T(4,128)S(1)}, u32[]{:S(2)}, u32[]{:S(2)}) async-start(f32[128,4,128]{2,1,0:T(4,128)} %bitcast.3), calls=%async_computation | async-start | bytes 524288 | tf_op jit(solution)/shard_map/all_to_all | solution.py:273
  15.0 8.2 %collective-permute-start.1 = (f32[8,256]{1,0:T(8,128)S(1)}, f32[8,256]{1,0:T(8,128)S(1)}, u32[]{:S(2)}, u32[]{:S(2)}) collective-permute-start(f32[8,256]{1,0:T(8,128)S(1)} %get-tuple-element.10), channel_id=1, source_target_pairs={{0,8},{8,16},{16,24},{24,32},{32,40},{40,48},{48,56},{56,64},{64,7... | collective-permute-start | bytes 24584 | tf_op jit(solution)/shard_map/ppermute | solution.py:276
  16.6 6.6 %collective-permute-start = (f32[8,256]{1,0:T(8,128)S(1)}, f32[8,256]{1,0:T(8,128)S(1)}, u32[]{:S(2)}, u32[]{:S(2)}) collective-permute-start(f32[8,256]{1,0:T(8,128)S(1)} %get-tuple-element.10), channel_id=1, source_target_pairs={{8,0},{16,8},{24,16},{32,24},{40,32},{48,40},{56,48},{64,56},{72,6... | collective-permute-start | bytes 24584 | tf_op jit(solution)/shard_map/ppermute | solution.py:277

commit v5 on v4

--- a/solution.py
+++ b/solution.py
@@ -134,7 +134,8 @@
     sides = edge_ref[...].T[0 : RY + 2 * SUB]
 
     rows, cols = RY + 2 * SUB, RX + 128
-    ends = jnp.where((iota((2 * SUB, RX), 0) < SUB) , inner_ref[...], outer_ref[...])
+    even = lax.rem(ty, 2) == 0
+    ends = jnp.where((iota((2 * SUB, RX), 0) < SUB) == even, inner_ref[...], outer_ref[...])
     field = jnp.concatenate(
         [jnp.concatenate([screen_ref[...], ends], axis=0), sides], axis=1
     )
@@ -273,8 +274,18 @@
         return lax.all_to_all(x, ("ty", "tx"), split_axis=0, concat_axis=0, tiled=True)
 
     got = exchange(send)
-    north = lax.ppermute(edges, "ty", [(i, (i + 1) % n_ty) for i in range(n_ty)])
-    south = lax.ppermute(edges, "ty", [((i + 1) % n_ty, i) for i in range(n_ty)])
+    def swap(first):
+        pairs = []
+        for y in range(n_ty):
+            other = y + 1 if (y - first) % 2 == 0 else y - 1
+            for x in range(n_tx):
+                if 0 <= other < n_ty:
+                    pairs.append((y * n_tx + x, other * n_tx + x))
+                else:
+                    pairs.append((y * n_tx + x, y * n_tx + (x ^ 1)))
+        return lax.ppermute(edges, ("ty", "tx"), pairs)
+
+    inner, outer = swap(0), swap(1)
     screen_next, reply = pl.pallas_call(
         lambda *refs: sample_kernel(n_ty, n_tx, *refs),
         out_shape=(shaped(RY, RX), shaped(tiles * 2 * CAP, 128)),
@@ -287,7 +298,7 @@
         ],
         compiler_params=PARAMS,
         name="step_and_sample",
-    )(screen, south, north, got)
+    )(screen, inner, outer, got)
     returned = exchange(reply)
     phases, slopes = pl.pallas_call(
         collect_kernel,

time: 47.5 us -> 46.5 us (0.979)
  starting transfers between devices: 17.1 us -> 14.5 us
  waiting for transfers between devices: 5.34 us -> 7.74 us
  blocking collectives: 19 us -> 18.1 us
    all_to_all x1, waiting for transfers between devices: 2.69 us -> 6.39 us  [exchange(): lax.all_to_all(x, ('ty', 'tx'), split_axis=0, concat_axis=0, tiled=True)]
    ppermute x2, starting transfers between devices: 5.57 us -> 3.04 us  [swap(): return lax.ppermute(edges, ('ty', 'tx'), pairs)]
    ppermute x2, waiting for transfers between devices: 2.66 us -> 1.35 us  [swap(): return lax.ppermute(edges, ('ty', 'tx'), pairs)]
    all_to_all x1, blocking collectives: 19 us -> 18.1 us  [exchange(): lax.all_to_all(x, ('ty', 'tx'), split_axis=0, concat_axis=0, tiled=True)]
where the time goes in v5:
time: 46.5 us; the launch traced here: 46.3 us
  blocking collectives  18.1 us (39%)
  starting transfers between devices  14.5 us (31%)
  waiting for transfers between devices  7.74 us (17%)
  Pallas kernels  4.48 us (10%)
  between operations  1.33 us (3%)
    all_to_all x1, blocking collectives, exchange(): lax.all_to_all(x, ('ty', 'tx'), split_axis=0, concat_axis=0, tiled=True)  18.1 us
    all_to_all x1, starting transfers between devices, exchange(): lax.all_to_all(x, ('ty', 'tx'), split_axis=0, concat_axis=0, tiled=True)  11.5 us
    all_to_all x1, waiting for transfers between devices, exchange(): lax.all_to_all(x, ('ty', 'tx'), split_axis=0, concat_axis=0, tiled=True)  6.39 us
    ppermute x2, starting transfers between devices, swap(): return lax.ppermute(edges, ('ty', 'tx'), pairs)  3.04 us
    pallas_call x1, Pallas kernels, local(): pl.pallas_call(lambda *refs: request_kernel(n_tx, *refs), out_shape=(shap...  2.19 us
    ppermute x2, waiting for transfers between devices, swap(): return lax.ppermute(edges, ('ty', 'tx'), pairs)  1.35 us
    pallas_call x1, Pallas kernels, local(): pl.pallas_call(lambda *refs: sample_kernel(n_ty, n_tx, *refs), out_shape=...  1.33 us
    pallas_call x1, Pallas kernels, local(): pl.pallas_call(collect_kernel, out_shape=(shaped(records, P_SIZE),) * 2,...  0.96 us
  transfers between devices with their start and end apart: 3, of which 2 were waited for; matrix products, arithmetic and copies ran while one was open for 0% of the time, Pallas kernels for 0%

profile of v5, /device:TPU:1, one launch (start us, length us, event | category | flops | bytes accessed | tf_op | source)
XLA Modules:
  0.0 46.3 jit_solution(15469300347995321691)
XLA Ops:
  0.6 0.0 copy-start.1
  1.3 0.0 copy-done.1
  1.3 2.2 %make_requests.1 = (f32[512,128]{1,0:T(8,128)}, f32[8,256]{1,0:T(8,128)S(1)}, s32[1,256]{1,0:T(1,128)S(4)}) custom-call(s32[1,1]{1,0:T(1,128)S(6)} %copy.9.refs_0_, s32[8,1,32]{2,1,0:T(1,128)S(1)} %bitcast.12, f32[64,256]{1,0:T(8,128)} %refs_0_.2, f32[2,16]{1,0:T(2,128)} %refs_3_.1, s32[8,32]{1,0:T(8,128)} %bitcast.14, f32[2,8,32]{2,1,0:T(8,128)} %bitcast.13), custom_call_target="tpu_custom_call" | custom-call | tf_op jit(solution)/shard_map/make_requests/pallas_call | solution.py:239
  3.5 0.0 copy-start
  3.5 11.5 %all-to-all-start = ((f32[128,4,128]{2,1,0:T(4,128)}), f32[128,4,128]{2,1,0:T(4,128)S(1)}, u32[]{:S(2)}, u32[]{:S(2)}) async-start(f32[128,4,128]{2,1,0:T(4,128)} %bitcast.3), calls=%async_computation | async-start | bytes 524288 | tf_op jit(solution)/shard_map/all_to_all | solution.py:274
  15.0 1.1 %collective-permute-start.1 = (f32[8,256]{1,0:T(8,128)S(1)}, f32[8,256]{1,0:T(8,128)S(1)}, u32[]{:S(2)}, u32[]{:S(2)}) collective-permute-start(f32[8,256]{1,0:T(8,128)S(1)} %get-tuple-element.10), channel_id=1, source_target_pairs={{0,1},{1,0},{2,3},{3,2},{4,5},{5,4},{6,7},{7,6},{8,16},{9,17},{10,... | collective-permute-start | bytes 24584 | tf_op jit(solution)/shard_map/ppermute | solution.py:286
  16.2 1.9 %collective-permute-start = (f32[8,256]{1,0:T(8,128)S(1)}, f32[8,256]{1,0:T(8,128)S(1)}, u32[]{:S(2)}, u32[]{:S(2)}) collective-permute-start(f32[8,256]{1,0:T(8,128)S(1)} %get-tuple-element.10), channel_id=1, source_target_pairs={{0,8},{1,9},{2,10},{3,11},{4,12},{5,13},{6,14},{7,15},{8,0},{9,1},... | collective-permute-start | bytes 24584 | tf_op jit(solution)/shard_map/ppermute | solution.py:286
  18.1 0.0 collective-permute-done.1.refs_2_
  18.1 1.3 %collective-permute-done.refs_1_ = f32[8,256]{1,0:T(8,128)S(1)} collective-permute-done((f32[8,256]{1,0:T(8,128)S(1)}, f32[8,256]{1,0:T(8,128)S(1)}, u32[]{:S(2)}, u32[]{:S(2)}) %collective-permute-start) | collective-permute-done | bytes 8224 | tf_op jit(solution)/shard_map/ppermute | solution.py:286
  19.4 6.4 %all-to-all-done = f32[128,4,128]{2,1,0:T(4,128)S(1)} async-done(((f32[128,4,128]{2,1,0:T(4,128)}), f32[128,4,128]{2,1,0:T(4,128)S(1)}, u32[]{:S(2)}, u32[]{:S(2)}) %all-to-all-start) | async-done | bytes 262176 | tf_op jit(solution)/shard_map/all_to_all | solution.py:274
  25.8 0.0 copy-done
  25.8 1.3 %step_and_sample.1 = (f32[64,256]{1,0:T(8,128)}, f32[1024,128]{1,0:T(8,128)S(1)}) custom-call(f32[64,256]{1,0:T(8,128)S(1)} %copy-done, f32[8,256]{1,0:T(8,128)S(1)} %collective-permute-done.refs_1_, f32[8,256]{1,0:T(8,128)S(1)} %collective-permute-done.1.refs_2_, f32[512,128]{1,0:T(8,128)S(1)} %bitcast.10), custom_call_target="tpu_custom_call" | custom-call | tf_op jit(solution)/shard_map/step_and_sample/pallas_call | solution.py:289
  27.2 18.1 %all_to_all.22 = f32[128,8,128]{2,1,0:T(8,128)S(1)} all-to-all(f32[128,8,128]{2,1,0:T(8,128)S(1)} %bitcast.11), channel_id=1, replica_groups=mesh['ty'=16,'tx'=8] {'ty','tx'}, dimensions={0} | all-to-all | bytes 1048576 | tf_op jit(solution)/shard_map/all_to_all | solution.py:274
  45.3 1.0 %collect.1 = (f32[256,128]{1,0:T(8,128)}, f32[256,128]{1,0:T(8,128)}) custom-call(s32[1,256]{1,0:T(1,128)S(4)} %get-tuple-element.13.slot_ref, f32[1024,128]{1,0:T(8,128)S(1)} %bitcast.9), custom_call_target="tpu_custom_call" | custom-call | tf_op jit(solution)/shard_map/collect/pallas_call | solution.py:303
Async XLA Ops:
  0.6 0.7 %copy-start.1 = (s32[1,1,8,32,1]{3,4,2,1,0:T(1,128)S(1)}, s32[1,1,8,32,1]{3,4,2,1,0:T(1,128)}, u32[]{:S(2)}) copy-start(s32[1,1,8,32,1]{3,4,2,1,0:T(1,128)} %param.9) | copy-start | bytes 3076
  3.5 22.3 %copy-start = (f32[64,256]{1,0:T(8,128)S(1)}, f32[64,256]{1,0:T(8,128)}, u32[]{:S(2)}) copy-start(f32[64,256]{1,0:T(8,128)} %refs_0_.2) | copy-start | bytes 196612
  3.5 22.3 %all-to-all-start = ((f32[128,4,128]{2,1,0:T(4,128)}), f32[128,4,128]{2,1,0:T(4,128)S(1)}, u32[]{:S(2)}, u32[]{:S(2)}) async-start(f32[128,4,128]{2,1,0:T(4,128)} %bitcast.3), calls=%async_computation | async-start | bytes 524288 | tf_op jit(solution)/shard_map/all_to_all | solution.py:274
  15.0 3.0 %collective-permute-start.1 = (f32[8,256]{1,0:T(8,128)S(1)}, f32[8,256]{1,0:T(8,128)S(1)}, u32[]{:S(2)}, u32[]{:S(2)}) collective-permute-start(f32[8,256]{1,0:T(8,128)S(1)} %get-tuple-element.10), channel_id=1, source_target_pairs={{0,1},{1,0},{2,3},{3,2},{4,5},{5,4},{6,7},{7,6},{8,16},{9,17},{10,... | collective-permute-start | bytes 24584 | tf_op jit(solution)/shard_map/ppermute | solution.py:286
  16.2 3.2 %collective-permute-start = (f32[8,256]{1,0:T(8,128)S(1)}, f32[8,256]{1,0:T(8,128)S(1)}, u32[]{:S(2)}, u32[]{:S(2)}) collective-permute-start(f32[8,256]{1,0:T(8,128)S(1)} %get-tuple-element.10), channel_id=1, source_target_pairs={{0,8},{1,9},{2,10},{3,11},{4,12},{5,13},{6,14},{7,15},{8,0},{9,1},... | collective-permute-start | bytes 24584 | tf_op jit(solution)/shard_map/ppermute | solution.py:286

commit v6 on v4

--- a/solution.py
+++ b/solution.py
@@ -43,7 +43,7 @@
     copies = [pltpu.make_async_copy(sources[i], refs[i], refs[4].at[i]) for i in range(4)]
     for copy in copies:
         copy.start()
-    screen_ref, table_ref, cell_ref, frac_ref = refs[:4]
+    cell_ref, frac_ref, table_ref, screen_ref = refs[:4]
     tx = lax.axis_index("tx")
     groups, width = tile_ref.shape[0], tile_ref.shape[2]
     records = groups * width
@@ -64,7 +64,7 @@
     picks = jnp.concatenate(
         [jnp.where(earlier == k, names, 0.0).astype(BF16) for k in range(CAP)], axis=0
     )
-    for copy in copies[2:]:
+    for copy in copies[:2]:
         copy.wait()
     cell = flat([cell_ref[s : s + 1, :] for s in range(groups)]).astype(F32)
     frac_row = flat([frac_ref[0, s : s + 1, :] for s in range(groups)])
@@ -83,7 +83,7 @@
     for k in range(1, CAP):
         requests = requests + pltpu.roll(found[k * tiles : (k + 1) * tiles], 4 * k, axis=1)
 
-    for copy in copies[:2]:
+    for copy in copies[2:]:
         copy.wait()
     edge_ref[...] = jnp.where(
         iota((2 * SUB, RX), 0) < SUB, screen_ref[0 : 2 * SUB, :], screen_ref[RY - 2 * SUB : RY, :]
@@ -110,7 +110,7 @@
 
 
 def sample_kernel(
-    n_ty, n_tx, screen_ref, inner_ref, outer_ref, got_ref, next_ref, reply_ref, edge_ref, tile_ref, sem
+    n_ty, n_tx, screen_ref, inner_ref, outer_ref, cross_ref, got_ref, next_ref, reply_ref, edge_ref, tile_ref, sem
 ):
     ty, tx = lax.axis_index("ty"), lax.axis_index("tx")
     tiles = n_ty * n_tx
@@ -134,7 +134,10 @@
     sides = edge_ref[...].T[0 : RY + 2 * SUB]
 
     rows, cols = RY + 2 * SUB, RX + 128
-    ends = jnp.where((iota((2 * SUB, RX), 0) < SUB) , inner_ref[...], outer_ref[...])
+    even = lax.rem(ty, 2) == 0
+    far_pair = lax.rem((ty + 1) // 2, 2) == 0
+    outer = jnp.where(far_pair, cross_ref[...], outer_ref[...])
+    ends = jnp.where((iota((2 * SUB, RX), 0) < SUB) == even, inner_ref[...], outer)
     field = jnp.concatenate(
         [jnp.concatenate([screen_ref[...], ends], axis=0), sides], axis=1
     )
@@ -247,10 +250,10 @@
         scratch_shapes=[
             pltpu.VMEM((1, records), jnp.int32),
             pltpu.SemaphoreType.DMA,
-            pltpu.VMEM((RY, RX), F32),
-            pltpu.VMEM(wind_table.shape, F32),
             pltpu.VMEM((groups, width), jnp.int32),
             pltpu.VMEM((2, groups, width), F32),
+            pltpu.VMEM(wind_table.shape, F32),
+            pltpu.VMEM((RY, RX), F32),
             pltpu.SemaphoreType.DMA((4,)),
         ],
         compiler_params=PARAMS,
@@ -261,10 +264,10 @@
         *[
             pltpu.with_memory_space_constraint(x, pltpu.HBM)
             for x in (
-                screen,
-                wind_table,
                 cell_index.reshape(groups, width),
                 fractions.reshape(2, groups, width),
+                wind_table,
+                screen,
             )
         ],
     )
@@ -273,12 +276,23 @@
         return lax.all_to_all(x, ("ty", "tx"), split_axis=0, concat_axis=0, tiled=True)
 
     got = exchange(send)
-    north = lax.ppermute(edges, "ty", [(i, (i + 1) % n_ty) for i in range(n_ty)])
-    south = lax.ppermute(edges, "ty", [((i + 1) % n_ty, i) for i in range(n_ty)])
+    def swap(firsts):
+        rows = {i: i + 1 for i in firsts if i + 1 < n_ty}
+        rows.update({j: i for i, j in rows.items()})
+        pairs = [
+            (y * n_tx + x, rows[y] * n_tx + x if y in rows else y * n_tx + (x ^ 1))
+            for y in range(n_ty)
+            for x in range(n_tx)
+        ]
+        return lax.ppermute(edges, ("ty", "tx"), pairs)
+
+    inner, outer, cross = [
+        swap(range(first, n_ty, step)) for first, step in ((0, 2), (1, 4), (3, 4))
+    ]
     screen_next, reply = pl.pallas_call(
         lambda *refs: sample_kernel(n_ty, n_tx, *refs),
         out_shape=(shaped(RY, RX), shaped(tiles * 2 * CAP, 128)),
-        in_specs=[VMEM] * 4,
+        in_specs=[VMEM] * 5,
         out_specs=(HBM, VMEM),
         scratch_shapes=[
             pltpu.VMEM((128, 128), F32),
@@ -287,7 +301,7 @@
         ],
         compiler_params=PARAMS,
         name="step_and_sample",
-    )(screen, south, north, got)
+    )(screen, inner, outer, cross, got)
     returned = exchange(reply)
     phases, slopes = pl.pallas_call(
         collect_kernel,

time: 47.5 us -> 46.5 us (0.979)
  starting transfers between devices: 17.1 us -> 14.9 us
  waiting for transfers between devices: 5.34 us -> 7.37 us
  blocking collectives: 19 us -> 18.2 us
    all_to_all x1, waiting for transfers between devices: 2.69 us -> 5.94 us  [exchange(): lax.all_to_all(x, ('ty', 'tx'), split_axis=0, concat_axis=0, tiled=True)]
    ppermute x2 -> x3, starting transfers between devices: 5.57 us -> 3.4 us  [swap(): return lax.ppermute(edges, ('ty', 'tx'), pairs)]
    ppermute x2 -> x3, waiting for transfers between devices: 2.66 us -> 1.43 us  [swap(): return lax.ppermute(edges, ('ty', 'tx'), pairs)]
    all_to_all x1, blocking collectives: 19 us -> 18.2 us  [exchange(): lax.all_to_all(x, ('ty', 'tx'), split_axis=0, concat_axis=0, tiled=True)]
  transfers between devices with their start and end apart: 3 -> 4, of which waited for: 2 -> 2; matrix products, arithmetic and copies ran while one was open for 0% -> 0% of each run, Pallas kernels for 0% -> 0%
where the time goes in v6:
time: 46.5 us; the launch traced here: 46.2 us
  blocking collectives  18.2 us (39%)
  starting transfers between devices  14.9 us (32%)
  waiting for transfers between devices  7.37 us (16%)
  Pallas kernels  4.44 us (10%)
  between operations  1.34 us (3%)
    all_to_all x1, blocking collectives, exchange(): lax.all_to_all(x, ('ty', 'tx'), split_axis=0, concat_axis=0, tiled=True)  18.2 us
    all_to_all x1, starting transfers between devices, exchange(): lax.all_to_all(x, ('ty', 'tx'), split_axis=0, concat_axis=0, tiled=True)  11.5 us
    all_to_all x1, waiting for transfers between devices, exchange(): lax.all_to_all(x, ('ty', 'tx'), split_axis=0, concat_axis=0, tiled=True)  5.94 us
    ppermute x3, starting transfers between devices, swap(): return lax.ppermute(edges, ('ty', 'tx'), pairs)  3.4 us
    pallas_call x1, Pallas kernels, local(): pl.pallas_call(lambda *refs: request_kernel(n_tx, *refs), out_shape=(shap...  2.15 us
    ppermute x3, waiting for transfers between devices, swap(): return lax.ppermute(edges, ('ty', 'tx'), pairs)  1.43 us
    pallas_call x1, Pallas kernels, local(): pl.pallas_call(lambda *refs: sample_kernel(n_ty, n_tx, *refs), out_shape=...  1.33 us
    pallas_call x1, Pallas kernels, local(): pl.pallas_call(collect_kernel, out_shape=(shaped(records, P_SIZE),) * 2,...  0.96 us
  transfers between devices with their start and end apart: 4, of which 2 were waited for; matrix products, arithmetic and copies ran while one was open for 0% of the time, Pallas kernels for 0%

profile of v6, /device:TPU:1, one launch (start us, length us, event | category | flops | bytes accessed | tf_op | source)
XLA Modules:
  0.0 46.2 jit_solution(9108916971749866412)
XLA Ops:
  0.6 0.0 copy-start.1
  1.3 0.0 copy-done.1
  1.3 2.1 %make_requests.1 = (f32[512,128]{1,0:T(8,128)}, f32[8,256]{1,0:T(8,128)S(1)}, s32[1,256]{1,0:T(1,128)S(4)}) custom-call(s32[1,1]{1,0:T(1,128)S(6)} %copy.9.refs_0_, s32[8,1,32]{2,1,0:T(1,128)S(1)} %bitcast.12, s32[8,32]{1,0:T(8,128)} %bitcast.14, f32[2,8,32]{2,1,0:T(8,128)} %bitcast.13, f32[2,16]{1,0:T(2,128)} %refs_4_.1, f32[64,256]{1,0:T(8,128)} %refs_0_.2), custom_call_target="tpu_custom_call" | custom-call | tf_op jit(solution)/shard_map/make_requests/pallas_call | solution.py:241
  3.5 0.0 copy-start
  3.5 11.5 %all-to-all-start = ((f32[128,4,128]{2,1,0:T(4,128)}), f32[128,4,128]{2,1,0:T(4,128)S(1)}, u32[]{:S(2)}, u32[]{:S(2)}) async-start(f32[128,4,128]{2,1,0:T(4,128)} %bitcast.3), calls=%async_computation | async-start | bytes 524288 | tf_op jit(solution)/shard_map/all_to_all | solution.py:276
  15.0 1.1 %collective-permute-start.2 = (f32[8,256]{1,0:T(8,128)S(1)}, f32[8,256]{1,0:T(8,128)S(1)}, u32[]{:S(2)}, u32[]{:S(2)}) collective-permute-start(f32[8,256]{1,0:T(8,128)S(1)} %get-tuple-element.10), channel_id=1, source_target_pairs={{0,1},{1,0},{2,3},{3,2},{4,5},{5,4},{6,7},{7,6},{8,9},{9,8},{10,11... | collective-permute-start | bytes 24584 | tf_op jit(solution)/shard_map/ppermute | solution.py:287
  16.1 0.1 collective-permute-start.1
  16.2 2.2 %collective-permute-start = (f32[8,256]{1,0:T(8,128)S(1)}, f32[8,256]{1,0:T(8,128)S(1)}, u32[]{:S(2)}, u32[]{:S(2)}) collective-permute-start(f32[8,256]{1,0:T(8,128)S(1)} %get-tuple-element.10), channel_id=1, source_target_pairs={{0,8},{1,9},{2,10},{3,11},{4,12},{5,13},{6,14},{7,15},{8,0},{9,1},... | collective-permute-start | bytes 24584 | tf_op jit(solution)/shard_map/ppermute | solution.py:287
  18.4 0.0 collective-permute-done.2.refs_3_
  18.4 0.0 collective-permute-done.1.refs_2_
  18.4 1.4 %collective-permute-done.refs_1_ = f32[8,256]{1,0:T(8,128)S(1)} collective-permute-done((f32[8,256]{1,0:T(8,128)S(1)}, f32[8,256]{1,0:T(8,128)S(1)}, u32[]{:S(2)}, u32[]{:S(2)}) %collective-permute-start) | collective-permute-done | bytes 8224 | tf_op jit(solution)/shard_map/ppermute | solution.py:287
  19.8 5.9 %all-to-all-done = f32[128,4,128]{2,1,0:T(4,128)S(1)} async-done(((f32[128,4,128]{2,1,0:T(4,128)}), f32[128,4,128]{2,1,0:T(4,128)S(1)}, u32[]{:S(2)}, u32[]{:S(2)}) %all-to-all-start) | async-done | bytes 262176 | tf_op jit(solution)/shard_map/all_to_all | solution.py:276
  25.8 0.0 copy-done
  25.8 1.3 %step_and_sample.1 = (f32[64,256]{1,0:T(8,128)}, f32[1024,128]{1,0:T(8,128)S(1)}) custom-call(f32[64,256]{1,0:T(8,128)S(1)} %copy-done, f32[8,256]{1,0:T(8,128)S(1)} %collective-permute-done.refs_1_, f32[8,256]{1,0:T(8,128)S(1)} %collective-permute-done.1.refs_2_, f32[8,256]{1,0:T(8,128)S(1)} %collective-permute-done.2.refs_3_, f32[512,128]{1,0:T(8,128)S(1)} %bitcast.10), custom_call_target="tpu_custom_call" | custom-call | tf_op jit(solution)/shard_map/step_and_sample/pallas_call | solution.py:292
  27.1 18.2 %all_to_all.22 = f32[128,8,128]{2,1,0:T(8,128)S(1)} all-to-all(f32[128,8,128]{2,1,0:T(8,128)S(1)} %bitcast.11), channel_id=1, replica_groups=mesh['ty'=16,'tx'=8] {'ty','tx'}, dimensions={0} | all-to-all | bytes 1048576 | tf_op jit(solution)/shard_map/all_to_all | solution.py:276
  45.3 1.0 %collect.1 = (f32[256,128]{1,0:T(8,128)}, f32[256,128]{1,0:T(8,128)}) custom-call(s32[1,256]{1,0:T(1,128)S(4)} %get-tuple-element.13.slot_ref, f32[1024,128]{1,0:T(8,128)S(1)} %bitcast.9), custom_call_target="tpu_custom_call" | custom-call | tf_op jit(solution)/shard_map/collect/pallas_call | solution.py:306
Async XLA Ops:
  0.6 0.7 %copy-start.1 = (s32[1,1,8,32,1]{3,4,2,1,0:T(1,128)S(1)}, s32[1,1,8,32,1]{3,4,2,1,0:T(1,128)}, u32[]{:S(2)}) copy-start(s32[1,1,8,32,1]{3,4,2,1,0:T(1,128)} %param.9) | copy-start | bytes 3076
  3.5 22.3 %copy-start = (f32[64,256]{1,0:T(8,128)S(1)}, f32[64,256]{1,0:T(8,128)}, u32[]{:S(2)}) copy-start(f32[64,256]{1,0:T(8,128)} %refs_0_.2) | copy-start | bytes 196612
  3.5 22.3 %all-to-all-start = ((f32[128,4,128]{2,1,0:T(4,128)}), f32[128,4,128]{2,1,0:T(4,128)S(1)}, u32[]{:S(2)}, u32[]{:S(2)}) async-start(f32[128,4,128]{2,1,0:T(4,128)} %bitcast.3), calls=%async_computation | async-start | bytes 524288 | tf_op jit(solution)/shard_map/all_to_all | solution.py:276
  15.0 3.4 %collective-permute-start.2 = (f32[8,256]{1,0:T(8,128)S(1)}, f32[8,256]{1,0:T(8,128)S(1)}, u32[]{:S(2)}, u32[]{:S(2)}) collective-permute-start(f32[8,256]{1,0:T(8,128)S(1)} %get-tuple-element.10), channel_id=1, source_target_pairs={{0,1},{1,0},{2,3},{3,2},{4,5},{5,4},{6,7},{7,6},{8,9},{9,8},{10,11... | collective-permute-start | bytes 24584 | tf_op jit(solution)/shard_map/ppermute | solution.py:287
  16.1 2.3 %collective-permute-start.1 = (f32[8,256]{1,0:T(8,128)S(1)}, f32[8,256]{1,0:T(8,128)S(1)}, u32[]{:S(2)}, u32[]{:S(2)}) collective-permute-start(f32[8,256]{1,0:T(8,128)S(1)} %get-tuple-element.10), channel_id=1, source_target_pairs={{0,1},{1,0},{2,3},{3,2},{4,5},{5,4},{6,7},{7,6},{8,16},{9,17},{10,... | collective-permute-start | bytes 24584 | tf_op jit(solution)/shard_map/ppermute | solution.py:287
  16.2 3.6 %collective-permute-start = (f32[8,256]{1,0:T(8,128)S(1)}, f32[8,256]{1,0:T(8,128)S(1)}, u32[]{:S(2)}, u32[]{:S(2)}) collective-permute-start(f32[8,256]{1,0:T(8,128)S(1)} %get-tuple-element.10), channel_id=1, source_target_pairs={{0,8},{1,9},{2,10},{3,11},{4,12},{5,13},{6,14},{7,15},{8,0},{9,1},... | collective-permute-start | bytes 24584 | tf_op jit(solution)/shard_map/ppermute | solution.py:287

commit v7 on v5

--- a/solution.py
+++ b/solution.py
@@ -12,8 +12,8 @@
 SUB = 4
 CAP = 4
 DIFFUSION = 0.2
-PARTS = 2
-UNROLL = 32
+PARTS = 4
+UNROLL = 64
 
 REC = 64
 F32 = jnp.float32
@@ -181,12 +181,14 @@
         row_k = jnp.floor((cell + 0.5) * (1.0 / SPAN))
         col_k = (cell - SPAN * row_k).astype(jnp.int32)
         row_k = jnp.concatenate([row_k, row_k[:, 0 : 3 * RY - 128]], axis=1)
-        upper, lower = [
-            jnp.dot(
-                jnp.where(line == row_k + d, 1.0, 0.0).astype(BF16), parts, preferred_element_type=F32
-            )
-            for d in (0.0, 1.0)
-        ]
+        picked = jnp.dot(
+            jnp.concatenate(
+                [jnp.where(line == row_k + d, 1.0, 0.0).astype(BF16) for d in (0.0, 1.0)], axis=0
+            ),
+            parts,
+            preferred_element_type=F32,
+        )
+        upper, lower = picked[0:tiles], picked[tiles:]
         far = lanes < col_k
         spot = (lanes + col_k) & 127
         upper, lower = [

time: 46.5 us -> 46.5 us (level)
  no operation moved by 1% of the time
where the time goes in v7:
time: 46.5 us; the launch traced here: 46.2 us
  blocking collectives  18.1 us (39%)
  starting transfers between devices  14.5 us (31%)
  waiting for transfers between devices  7.74 us (17%)
  Pallas kernels  4.44 us (10%)
  between operations  1.33 us (3%)
    all_to_all x1, blocking collectives, exchange(): lax.all_to_all(x, ('ty', 'tx'), split_axis=0, concat_axis=0, tiled=True)  18.1 us
    all_to_all x1, starting transfers between devices, exchange(): lax.all_to_all(x, ('ty', 'tx'), split_axis=0, concat_axis=0, tiled=True)  11.5 us
    all_to_all x1, waiting for transfers between devices, exchange(): lax.all_to_all(x, ('ty', 'tx'), split_axis=0, concat_axis=0, tiled=True)  6.39 us
    ppermute x2, starting transfers between devices, swap(): return lax.ppermute(edges, ('ty', 'tx'), pairs)  3.04 us
    pallas_call x1, Pallas kernels, local(): pl.pallas_call(lambda *refs: request_kernel(n_tx, *refs), out_shape=(shap...  2.19 us
    ppermute x2, waiting for transfers between devices, swap(): return lax.ppermute(edges, ('ty', 'tx'), pairs)  1.35 us
    pallas_call x1, Pallas kernels, local(): pl.pallas_call(lambda *refs: sample_kernel(n_ty, n_tx, *refs), out_shape=...  1.32 us
    pallas_call x1, Pallas kernels, local(): pl.pallas_call(collect_kernel, out_shape=(shaped(records, P_SIZE),) * 2,...  0.93 us
  transfers between devices with their start and end apart: 3, of which 2 were waited for; matrix products, arithmetic and copies ran while one was open for 0% of the time, Pallas kernels for 0%

profile of v7, /device:TPU:1, one launch (start us, length us, event | category | flops | bytes accessed | tf_op | source)
XLA Modules:
  0.0 46.2 jit_solution(10626931382040097664)
XLA Ops:
  0.6 0.0 copy-start.1
  1.3 0.0 copy-done.1
  1.3 2.2 %make_requests.1 = (f32[512,128]{1,0:T(8,128)}, f32[8,256]{1,0:T(8,128)S(1)}, s32[1,256]{1,0:T(1,128)S(4)}) custom-call(s32[1,1]{1,0:T(1,128)S(6)} %copy.9.refs_0_, s32[8,1,32]{2,1,0:T(1,128)S(1)} %bitcast.12, f32[64,256]{1,0:T(8,128)} %refs_0_.2, f32[2,16]{1,0:T(2,128)} %refs_3_.1, s32[8,32]{1,0:T(8,128)} %bitcast.14, f32[2,8,32]{2,1,0:T(8,128)} %bitcast.13), custom_call_target="tpu_custom_call" | custom-call | tf_op jit(solution)/shard_map/make_requests/pallas_call | solution.py:241
  3.5 0.0 copy-start
  3.5 11.5 %all-to-all-start = ((f32[128,4,128]{2,1,0:T(4,128)}), f32[128,4,128]{2,1,0:T(4,128)S(1)}, u32[]{:S(2)}, u32[]{:S(2)}) async-start(f32[128,4,128]{2,1,0:T(4,128)} %bitcast.3), calls=%async_computation | async-start | bytes 524288 | tf_op jit(solution)/shard_map/all_to_all | solution.py:276
  15.0 1.1 %collective-permute-start.1 = (f32[8,256]{1,0:T(8,128)S(1)}, f32[8,256]{1,0:T(8,128)S(1)}, u32[]{:S(2)}, u32[]{:S(2)}) collective-permute-start(f32[8,256]{1,0:T(8,128)S(1)} %get-tuple-element.10), channel_id=1, source_target_pairs={{0,1},{1,0},{2,3},{3,2},{4,5},{5,4},{6,7},{7,6},{8,16},{9,17},{10,... | collective-permute-start | bytes 24584 | tf_op jit(solution)/shard_map/ppermute | solution.py:288
  16.2 1.9 %collective-permute-start = (f32[8,256]{1,0:T(8,128)S(1)}, f32[8,256]{1,0:T(8,128)S(1)}, u32[]{:S(2)}, u32[]{:S(2)}) collective-permute-start(f32[8,256]{1,0:T(8,128)S(1)} %get-tuple-element.10), channel_id=1, source_target_pairs={{0,8},{1,9},{2,10},{3,11},{4,12},{5,13},{6,14},{7,15},{8,0},{9,1},... | collective-permute-start | bytes 24584 | tf_op jit(solution)/shard_map/ppermute | solution.py:288
  18.1 0.0 collective-permute-done.1.refs_2_
  18.1 1.3 %collective-permute-done.refs_1_ = f32[8,256]{1,0:T(8,128)S(1)} collective-permute-done((f32[8,256]{1,0:T(8,128)S(1)}, f32[8,256]{1,0:T(8,128)S(1)}, u32[]{:S(2)}, u32[]{:S(2)}) %collective-permute-start) | collective-permute-done | bytes 8224 | tf_op jit(solution)/shard_map/ppermute | solution.py:288
  19.4 6.4 %all-to-all-done = f32[128,4,128]{2,1,0:T(4,128)S(1)} async-done(((f32[128,4,128]{2,1,0:T(4,128)}), f32[128,4,128]{2,1,0:T(4,128)S(1)}, u32[]{:S(2)}, u32[]{:S(2)}) %all-to-all-start) | async-done | bytes 262176 | tf_op jit(solution)/shard_map/all_to_all | solution.py:276
  25.8 0.0 copy-done
  25.8 1.3 %step_and_sample.1 = (f32[64,256]{1,0:T(8,128)}, f32[1024,128]{1,0:T(8,128)S(1)}) custom-call(f32[64,256]{1,0:T(8,128)S(1)} %copy-done, f32[8,256]{1,0:T(8,128)S(1)} %collective-permute-done.refs_1_, f32[8,256]{1,0:T(8,128)S(1)} %collective-permute-done.1.refs_2_, f32[512,128]{1,0:T(8,128)S(1)} %bitcast.10), custom_call_target="tpu_custom_call" | custom-call | tf_op jit(solution)/shard_map/step_and_sample/pallas_call | solution.py:291
  27.1 18.1 %all_to_all.22 = f32[128,8,128]{2,1,0:T(8,128)S(1)} all-to-all(f32[128,8,128]{2,1,0:T(8,128)S(1)} %bitcast.11), channel_id=1, replica_groups=mesh['ty'=16,'tx'=8] {'ty','tx'}, dimensions={0} | all-to-all | bytes 1048576 | tf_op jit(solution)/shard_map/all_to_all | solution.py:276
  45.3 0.9 %collect.1 = (f32[256,128]{1,0:T(8,128)}, f32[256,128]{1,0:T(8,128)}) custom-call(s32[1,256]{1,0:T(1,128)S(4)} %get-tuple-element.13.slot_ref, f32[1024,128]{1,0:T(8,128)S(1)} %bitcast.9), custom_call_target="tpu_custom_call" | custom-call | tf_op jit(solution)/shard_map/collect/pallas_call | solution.py:305
Async XLA Ops:
  0.6 0.7 %copy-start.1 = (s32[1,1,8,32,1]{3,4,2,1,0:T(1,128)S(1)}, s32[1,1,8,32,1]{3,4,2,1,0:T(1,128)}, u32[]{:S(2)}) copy-start(s32[1,1,8,32,1]{3,4,2,1,0:T(1,128)} %param.9) | copy-start | bytes 3076
  3.5 22.3 %copy-start = (f32[64,256]{1,0:T(8,128)S(1)}, f32[64,256]{1,0:T(8,128)}, u32[]{:S(2)}) copy-start(f32[64,256]{1,0:T(8,128)} %refs_0_.2) | copy-start | bytes 196612
  3.5 22.3 %all-to-all-start = ((f32[128,4,128]{2,1,0:T(4,128)}), f32[128,4,128]{2,1,0:T(4,128)S(1)}, u32[]{:S(2)}, u32[]{:S(2)}) async-start(f32[128,4,128]{2,1,0:T(4,128)} %bitcast.3), calls=%async_computation | async-start | bytes 524288 | tf_op jit(solution)/shard_map/all_to_all | solution.py:276
  15.0 3.0 %collective-permute-start.1 = (f32[8,256]{1,0:T(8,128)S(1)}, f32[8,256]{1,0:T(8,128)S(1)}, u32[]{:S(2)}, u32[]{:S(2)}) collective-permute-start(f32[8,256]{1,0:T(8,128)S(1)} %get-tuple-element.10), channel_id=1, source_target_pairs={{0,1},{1,0},{2,3},{3,2},{4,5},{5,4},{6,7},{7,6},{8,16},{9,17},{10,... | collective-permute-start | bytes 24584 | tf_op jit(solution)/shard_map/ppermute | solution.py:288
  16.2 3.2 %collective-permute-start = (f32[8,256]{1,0:T(8,128)S(1)}, f32[8,256]{1,0:T(8,128)S(1)}, u32[]{:S(2)}, u32[]{:S(2)}) collective-permute-start(f32[8,256]{1,0:T(8,128)S(1)} %get-tuple-element.10), channel_id=1, source_target_pairs={{0,8},{1,9},{2,10},{3,11},{4,12},{5,13},{6,14},{7,15},{8,0},{9,1},... | collective-permute-start | bytes 24584 | tf_op jit(solution)/shard_map/ppermute | solution.py:288
